TPU v7x, 128 devices: a whole 4x4x4 slice. The times are simulated.
128 devices in a mesh: aa: 8 (over x, core), ba: 16 (over y, z).
Axes of the slice: x: 4, y: 4, z: 4, core: 2. Of those that a mesh axis runs over, the one named last changes fastest.
Arguments:
- rotation_harmonics: bfloat16 [32, 2, 819840], P('ba', None, 'aa'), may hold values from -2048 to 2048
- dilation_harmonics: bfloat16 [32, 2, 819840], P('ba', None, 'aa'), may hold values from -2048 to 2048
- thermal_harmonics: bfloat16 [32, 2, 819840], P('ba', None, 'aa'), may hold values from -3 to 3
- associated_polynomials: bfloat16 [48, 819840], P(None, 'aa'), may hold values from -0.0068359375 to 0.0068359375
- harmonic_order_list: int32 [8, 160], replicated, may hold values from 0 to 1279, as said below
- meridian_counts: int32 [96], replicated, may hold values from 20 to 5136, as said below
- latitude_limits: int32 [9], replicated, may hold values from 0 to 96, as said below
Outputs:
- zonal_velocity_mesh: float32 [32, 128, 6144], P(None, 'aa', 'ba')
- meridional_velocity_mesh: float32 [32, 128, 6144], P(None, 'aa', 'ba')
- temp_grid: float32 [32, 128, 6144], P(None, 'aa', 'ba')
Inputs may be any that keep to these rules, and one draw needn't show every extreme that they name: `harmonic_order_list`: row a lists the wavenumbers of index a of aa as 80 pairs: entry 2j is some p below 640 and entry 2j+1 is 1279-p; every wavenumber stands once in the whole array. `meridian_counts`: window latitudes run from north to south: the first 48 have 20 + 4 j points for distinct rising j below 1280, the last 48 repeat these counts in reverse order, and the largest count is 5136. `latitude_limits`: the first entry is 0 and the last 96; entries rise; each band holds 1 to 16 latitudes and one band holds exactly 16.
All inputs are finite; a program needn't handle non-finite values.
Results may differ from a plain program's by a relative error of at most 0.0047.
Values may be sent and summed in bfloat16 or wider, within the bound.
No kernel may reach another device: no remote copies, remote signals or barrier semaphores. Data moves between devices by JAX's collectives and lax.ppermute only.
A program may use at most 192 MiB of HBM per device.

v0:
```python
import math

import jax
import jax.numpy as jnp
from jax import lax
from jax.sharding import PartitionSpec as P

MW = 1280
BAND_MAX = 16
NLON_MAX = 5136


full_turn = 2.0 * math.pi


def pair_layout(lower_waves):
    position = jnp.arange(MW + 1, dtype=jnp.int32)
    first_seg = position[None, :] < (MW - lower_waves)[:, None]
    wavenum = jnp.where(first_seg, lower_waves[:, None], MW - 1 - lower_waves[:, None])
    degree = jnp.where(first_seg, lower_waves[:, None] + position[None, :], position[None, :] - 1)
    return (first_seg, wavenum, degree)


def shift_down(values):
    return jnp.concatenate([jnp.zeros_like(values[..., :1]), values[..., :-1]], axis=-1)


def shift_up(values):
    return jnp.concatenate([values[..., 1:], jnp.zeros_like(values[..., :1])], axis=-1)


def times_i(values):
    return jnp.stack([-values[:, 1], values[:, 0]], axis=1)


def spectral_winds(curl_field, spread_field, first_seg, wavenum, degree):
    order_m = wavenum.astype(jnp.float32)
    order_n = degree.astype(jnp.float32)
    denom = jnp.maximum(order_n * (order_n + 1.0), 1.0)
    stream = jnp.where(degree > 0, -curl_field.astype(jnp.float32) / denom, 0.0)
    potential = jnp.where(degree > 0, -spread_field.astype(jnp.float32) / denom, 0.0)
    coupling = jnp.sqrt(
        jnp.maximum((order_n * order_n - order_m * order_m) / (4.0 * order_n * order_n - 1.0), 0.0)
    )
    seg_flag = first_seg.astype(jnp.int32)
    same_seg = (seg_flag == shift_up(seg_flag)).astype(jnp.float32)
    coupling_up = shift_up(coupling) * same_seg
    lower = (order_n - 1.0) * coupling
    upper = (order_n + 2.0) * coupling_up
    zonal_velocity_mesh = (
        lower * shift_down(stream) - upper * shift_up(stream) + order_m * times_i(potential)
    )
    meridional_velocity_mesh = (
        -lower * shift_down(potential) + upper * shift_up(potential) + order_m * times_i(stream)
    )
    return (zonal_velocity_mesh.astype(jnp.bfloat16), meridional_velocity_mesh.astype(jnp.bfloat16))


def legendre_products(poly_table, spectral_inputs, first_seg, lower_waves):
    spectra_t = jnp.transpose(spectral_inputs, (3, 4, 2, 0, 1))
    pair_count = spectra_t.shape[0]
    half_width = (spectra_t.shape[1] + 1) // 2
    north_count = poly_table.shape[0]
    padded_data = jnp.concatenate([spectra_t, jnp.zeros_like(spectra_t[:, :1])], axis=1)
    data = padded_data.reshape((pair_count, half_width, 2) + spectra_t.shape[2:])
    padded_seg = jnp.concatenate([first_seg, jnp.zeros_like(first_seg[:, :1])], axis=1).reshape(
        pair_count, half_width, 2
    )
    seg_mask = jnp.stack([padded_seg, jnp.logical_not(padded_seg)], axis=-1).astype(jnp.bfloat16)
    table = poly_table.reshape(north_count, pair_count, -1)
    table = jnp.concatenate([table, jnp.zeros_like(table[:, :, :1])], axis=2).reshape(
        north_count, pair_count, half_width, 2
    )
    masked_table = table[..., None] * seg_mask[None]
    products = jnp.einsum(
        "pthes,thexyz->tpsexyz", masked_table, data, preferred_element_type=jnp.float32
    )
    odd_lower = lower_waves % 2 == 1
    second = jnp.where(
        odd_lower[:, None, None, None, None, None], products[:, :, 1, ::-1], products[:, :, 1]
    )
    products = jnp.stack([products[:, :, 0], second], axis=2)
    return products.reshape(pair_count, north_count, -1)


def fold_hemispheres(transform_output, level_count):
    shaped = transform_output.reshape(
        transform_output.shape[0], transform_output.shape[1], 2, 2, 2, 3, level_count
    )
    northern = shaped[:, :, :, 0] + shaped[:, :, :, 1]
    southern = shaped[:, :, :, 0] - shaped[:, :, :, 1]
    return jnp.concatenate([northern, southern[:, ::-1]], axis=1).astype(jnp.bfloat16)


def trig_table(wave_table, longitudes, lon_count, occupied):
    residue = wave_table[:, :, None] * longitudes[None, None, :] % lon_count
    angles = residue.astype(jnp.float32) * full_turn / lon_count.astype(jnp.float32)
    active = (
        occupied
        & (longitudes[None, None, :] < lon_count)
        & (wave_table[:, :, None] <= (lon_count - 1) // 2)
    )
    weights = (jnp.where(wave_table == 0, 1.0, 2.0)[:, :, None] * active).astype(jnp.bfloat16)
    cosine = jnp.cos(angles).astype(jnp.bfloat16) * weights
    sine_part = (-jnp.sin(angles)).astype(jnp.bfloat16) * weights
    return jnp.stack([cosine, sine_part], axis=1)


def per_device(
    rotation_harmonics,
    dilation_harmonics,
    thermal_harmonics,
    associated_polynomials,
    harmonic_order_list,
    meridian_counts,
    latitude_limits,
):
    band_count = lax.axis_size("aa")
    piece_count = lax.axis_size("ba")
    band_index = lax.axis_index("aa")
    piece_index = lax.axis_index("ba")
    level_count = rotation_harmonics.shape[0]
    coef_count = rotation_harmonics.shape[2]
    width = MW + 1
    pair_count = coef_count // width
    window = meridian_counts.shape[0]
    wave_row = lax.dynamic_slice_in_dim(harmonic_order_list, band_index, 1, 0)[0]
    lower_waves = wave_row[0::2]
    first_seg, wavenum, degree = pair_layout(lower_waves)

    def hemisphere_couples(field):
        return field.reshape(level_count, 2, pair_count, width)

    zonal_velocity_mesh, meridional_velocity_mesh = spectral_winds(
        hemisphere_couples(rotation_harmonics),
        hemisphere_couples(dilation_harmonics),
        first_seg,
        wavenum,
        degree,
    )
    spectral_inputs = jnp.stack(
        [zonal_velocity_mesh, meridional_velocity_mesh, hemisphere_couples(thermal_harmonics)],
        axis=0,
    )
    transform_output = legendre_products(
        associated_polynomials, spectral_inputs, first_seg, lower_waves
    )
    azimuthal_harmonics = fold_hemispheres(transform_output, level_count)
    padded = jnp.concatenate(
        [
            azimuthal_harmonics,
            jnp.zeros((pair_count, BAND_MAX) + azimuthal_harmonics.shape[2:], jnp.bfloat16),
        ],
        axis=1,
    )

    def band_rows(first_row):
        return lax.dynamic_slice_in_dim(padded, first_row, BAND_MAX, 1)

    outgoing = jax.vmap(band_rows)(latitude_limits[:-1])
    outgoing = jnp.transpose(outgoing, (0, 2, 4, 5, 6, 1, 3)).reshape(
        band_count, BAND_MAX, 2, 3 * level_count, 2 * pair_count
    )
    incoming = lax.all_to_all(outgoing, "aa", split_axis=0, concat_axis=0, tiled=True)
    band_edges = lax.dynamic_slice_in_dim(latitude_limits, band_index, 2, 0)
    slot_index = jnp.arange(BAND_MAX, dtype=jnp.int32)
    latitude = band_edges[0] + slot_index
    occupied = latitude < band_edges[1]
    matches = jnp.arange(window, dtype=jnp.int32)[None, :] == latitude[:, None]
    lon_counts = jnp.sum(jnp.where(matches, meridian_counts[None, :], 0), axis=1)
    lon_counts = jnp.where(occupied, lon_counts, 1)
    piece_width = (NLON_MAX + 128 * piece_count - 1) // (128 * piece_count) * 128
    longitudes = jnp.arange(piece_width, dtype=jnp.int32) * piece_count + piece_index

    def one_slot(inputs):
        lon_count, live = inputs
        return trig_table(harmonic_order_list, longitudes, lon_count, live)

    tables = lax.map(one_slot, (lon_counts, occupied))
    gathered = lax.all_gather(incoming, "ba", axis=3, tiled=True)
    values = jnp.einsum("asrgk,sarkx->sgx", gathered, tables, preferred_element_type=jnp.float32)
    values = values.reshape(BAND_MAX, piece_count, 3, level_count, piece_width)
    values = jnp.transpose(values, (0, 2, 1, 3, 4)).reshape(
        BAND_MAX, 3, piece_count * level_count, piece_width
    )
    outputs = jnp.transpose(values, (1, 2, 0, 3))
    return (outputs[0], outputs[1], outputs[2])


def solution(mesh):
    return jax.shard_map(
        per_device,
        mesh=mesh,
        in_specs=(
            P("ba", None, "aa"),
            P("ba", None, "aa"),
            P("ba", None, "aa"),
            P(None, "aa"),
            P(),
            P(),
            P(),
        ),
        out_specs=(P(None, "aa", "ba"), P(None, "aa", "ba"), P(None, "aa", "ba")),
        check_vma=False,
    )
```

profile of v0, /device:TPU:0, one launch (start us, length us, event | category | flops | bytes accessed | tf_op | source)
XLA Modules:
  0.0 822.6 jit_solution(9474705931984014567)
XLA Ops:
  9.3 1.9 add_multiply_fusion.1
  12.9 3.0 neg.44
  15.9 4.5 copy.53
  20.4 3.1 convert_negate_fusion.1
  23.4 4.1 neg.42
  27.5 5.1 copy.52
  32.6 7.7 divide_select_fusion
  40.3 3.5 slice_negate_fusion
  43.9 5.5 fusion.46
  52.0 3.1 stack_reshape.4
  55.1 2.8 copy.55
  59.2 1.4 slice.98
  61.0 14.3 %fusion.30 = (bf16[1,2,2,80,1281]{3,1,0,2,4:T(2,128)(2,1)S(1)}, bf16[1,2,2,80,1281]{3,1,0,2,4:T(2,128)(2,1)S(1)}) fusion(f32[2,1,80,1281]{2,0,1,3:T(2,128)} %get-tuple-element.161, f32[2,1,80,1281]{2,0,1,3:T(2,128)} %get-tuple-element.162, f32[80,1281]{0,1:T(8,128)S(1)} %copy-done.3, f32[2,2,80,1280]{2,0,1,3:T(2,128)S(1)} %copy-done, ...), kind=kLoop, calls=%fused_computation.48 | loop fusion | flops 5738880 | bytes 13112320 | tf_op jit(solution)/shard_map/stack | solution.py:141
  75.3 5.5 maximum_bitcast_fusion.1
  80.8 5.9 concatenate.50
  86.7 16.0 %copy.71 = bf16[80,641,2,2,3,2,1]{1,4,6,5,3,2,0:T(4,128)(2,1)} copy(bf16[80,641,2,2,3,2,1]{0,5,4,3,2,1,6:T(2,128)(2,1)} %bitcast.74) | data formatting | bytes 4922880 | tf_op jit(solution)/shard_map/reshape | solution.py:65
  103.5 18.6 %reshape.377 = bf16[48,80,1281]{2,1,0:T(8,128)(2,1)} reshape(bf16[48,102480]{1,0:T(8,128)(2,1)} %param.12) | data formatting | bytes 19676160 | tf_op jit(solution)/shard_map/reshape | solution.py:70
  122.1 19.9 %copy.56 = bf16[48,80,1281]{1,0,2:T(8,128)(2,1)} copy(bf16[48,80,1281]{2,1,0:T(8,128)(2,1)} %reshape.377) | data formatting | bytes 19676160 | tf_op jit(solution)/shard_map/reshape | solution.py:70
  142.0 14.3 %concatenate.51 = bf16[48,80,1282]{1,0,2:T(8,128)(2,1)} pad(bf16[48,80,1281]{1,0,2:T(8,128)(2,1)} %copy.56, bf16[]{:T(256)} %constant.131.clone.1), padding=0_0x0_0x0_1 | pad | bytes 19683842 | tf_op jit(solution)/shard_map/concatenate | solution.py:71
  156.3 24.4 %copy.57 = bf16[48,80,641,2]{2,0,3,1:T(8,128)(2,1)} copy(bf16[48,80,641,2]{1,0,3,2:T(8,128)(2,1)} %bitcast.73) | data formatting | bytes 19691520 | tf_op jit(solution)/shard_map/mul | solution.py:74
  180.7 15.2 %fusion.23 = f32[80,48,2,2,2,3,2]{1,5,2,6,4,3,0:T(4,128)S(1)} fusion(bf16[80,641,2,2,3,2,1]{1,4,6,5,3,2,0:T(4,128)(2,1)} %copy.71, bf16[80,641,2,2]{1,3,2,0:T(2,128)(2,1)S(1)} %copy.60, bf16[48,80,641,2]{2,0,3,1:T(8,128)(2,1)} %copy.57), kind=kOutput, calls=%fused_computation.41 | convolution fusion | flops 275681280 | bytes 13454720 | tf_op jit(solution)/shard_map/pthes,thexyz->tpsexyz/dot_general | solution.py:75
  198.3 2.0 rev.7
  202.7 1.5 gather_fusion
  204.2 4.4 copy.66
  208.6 5.1 copy.67
  213.7 4.5 all-to-all-start
  221.0 10.4 %all-to-all-done = bf16[8,16,2,6,160]{4,1,3,2,0:T(8,128)(2,1)S(1)} async-done(((bf16[8,16,2,6,160]{4,1,3,2,0:T(8,128)(2,1)}), bf16[8,16,2,6,160]{4,1,3,2,0:T(8,128)(2,1)S(1)}, u32[]{:S(2)}, u32[]{:S(2)}) %all-to-all-start) | async-done | bytes 491552 | tf_op jit(solution)/shard_map/all_to_all | solution.py:164
  232.4 546.8 %while.14 = (s32[]{:T(128)}, bf16[16,8,2,160,384]{4,3,2,1,0:T(8,128)(2,1)}, s32[8,160]{1,0:T(8,128)S(1)}, s32[16]{0:T(128)S(1)}, pred[16]{0:T(512)(128)(4,1)S(1)...) while((s32[]{:T(128)}, bf16[16,8,2,160,384]{4,3,2,1,0:T(8,128)(2,1)}, ...), condition=%wide.region_2.3_spmd.clone, body=%wide.region_1.2_spmd.clone.sunk | while | flops 15243286 | bytes 5925470 | solution.py:179
  237.6 27.5 %fusion.54 = (bf16[8,1,160,384]{3,2,1,0:T(8,128)(2,1)S(1)}, bf16[8,1,160,384]{3,2,1,0:T(8,128)(2,1)S(1)}) fusion(bf16[8,160]{1,0:T(8,128)(2,1)S(1)} %compare_select_fusion.5, pred[8,160]{1,0:T(8,128)(4,1)S(1)} %broadcast_compare_fusion.4, pred[384]{0:T(512)(128)(4,1)S(1)} %compare_and_fusion.2, f32[]{:T(128)S(6)} %convert_element_type.197, ...), kind=kLoop, calls=%fused_computation.17.clone.1 | loop fusion | flops 11304960 | bytes 1976969 | tf_op jit(solution)/shard_map/while/body/eval_jaxpr/mul | solution.py:104
  265.1 1.6 fusion.55
  271.8 27.5 %fusion.54 = (bf16[8,1,160,384]{3,2,1,0:T(8,128)(2,1)S(1)}, bf16[8,1,160,384]{3,2,1,0:T(8,128)(2,1)S(1)}) fusion(bf16[8,160]{1,0:T(8,128)(2,1)S(1)} %compare_select_fusion.5, pred[8,160]{1,0:T(8,128)(4,1)S(1)} %broadcast_compare_fusion.4, pred[384]{0:T(512)(128)(4,1)S(1)} %compare_and_fusion.2, f32[]{:T(128)S(6)} %convert_element_type.197, ...), kind=kLoop, calls=%fused_computation.17.clone.1 | loop fusion | flops 11304960 | bytes 1976969 | tf_op jit(solution)/shard_map/while/body/eval_jaxpr/mul | solution.py:104
  299.3 1.5 fusion.55
  305.9 27.5 %fusion.54 = (bf16[8,1,160,384]{3,2,1,0:T(8,128)(2,1)S(1)}, bf16[8,1,160,384]{3,2,1,0:T(8,128)(2,1)S(1)}) fusion(bf16[8,160]{1,0:T(8,128)(2,1)S(1)} %compare_select_fusion.5, pred[8,160]{1,0:T(8,128)(4,1)S(1)} %broadcast_compare_fusion.4, pred[384]{0:T(512)(128)(4,1)S(1)} %compare_and_fusion.2, f32[]{:T(128)S(6)} %convert_element_type.197, ...), kind=kLoop, calls=%fused_computation.17.clone.1 | loop fusion | flops 11304960 | bytes 1976969 | tf_op jit(solution)/shard_map/while/body/eval_jaxpr/mul | solution.py:104
  333.4 1.5 fusion.55
  340.1 27.5 %fusion.54 = (bf16[8,1,160,384]{3,2,1,0:T(8,128)(2,1)S(1)}, bf16[8,1,160,384]{3,2,1,0:T(8,128)(2,1)S(1)}) fusion(bf16[8,160]{1,0:T(8,128)(2,1)S(1)} %compare_select_fusion.5, pred[8,160]{1,0:T(8,128)(4,1)S(1)} %broadcast_compare_fusion.4, pred[384]{0:T(512)(128)(4,1)S(1)} %compare_and_fusion.2, f32[]{:T(128)S(6)} %convert_element_type.197, ...), kind=kLoop, calls=%fused_computation.17.clone.1 | loop fusion | flops 11304960 | bytes 1976969 | tf_op jit(solution)/shard_map/while/body/eval_jaxpr/mul | solution.py:104
  367.6 1.5 fusion.55
  374.2 27.5 %fusion.54 = (bf16[8,1,160,384]{3,2,1,0:T(8,128)(2,1)S(1)}, bf16[8,1,160,384]{3,2,1,0:T(8,128)(2,1)S(1)}) fusion(bf16[8,160]{1,0:T(8,128)(2,1)S(1)} %compare_select_fusion.5, pred[8,160]{1,0:T(8,128)(4,1)S(1)} %broadcast_compare_fusion.4, pred[384]{0:T(512)(128)(4,1)S(1)} %compare_and_fusion.2, f32[]{:T(128)S(6)} %convert_element_type.197, ...), kind=kLoop, calls=%fused_computation.17.clone.1 | loop fusion | flops 11304960 | bytes 1976969 | tf_op jit(solution)/shard_map/while/body/eval_jaxpr/mul | solution.py:104
  401.7 1.6 fusion.55
  408.5 27.5 %fusion.54 = (bf16[8,1,160,384]{3,2,1,0:T(8,128)(2,1)S(1)}, bf16[8,1,160,384]{3,2,1,0:T(8,128)(2,1)S(1)}) fusion(bf16[8,160]{1,0:T(8,128)(2,1)S(1)} %compare_select_fusion.5, pred[8,160]{1,0:T(8,128)(4,1)S(1)} %broadcast_compare_fusion.4, pred[384]{0:T(512)(128)(4,1)S(1)} %compare_and_fusion.2, f32[]{:T(128)S(6)} %convert_element_type.197, ...), kind=kLoop, calls=%fused_computation.17.clone.1 | loop fusion | flops 11304960 | bytes 1976969 | tf_op jit(solution)/shard_map/while/body/eval_jaxpr/mul | solution.py:104
  435.9 1.5 fusion.55
  442.6 27.5 %fusion.54 = (bf16[8,1,160,384]{3,2,1,0:T(8,128)(2,1)S(1)}, bf16[8,1,160,384]{3,2,1,0:T(8,128)(2,1)S(1)}) fusion(bf16[8,160]{1,0:T(8,128)(2,1)S(1)} %compare_select_fusion.5, pred[8,160]{1,0:T(8,128)(4,1)S(1)} %broadcast_compare_fusion.4, pred[384]{0:T(512)(128)(4,1)S(1)} %compare_and_fusion.2, f32[]{:T(128)S(6)} %convert_element_type.197, ...), kind=kLoop, calls=%fused_computation.17.clone.1 | loop fusion | flops 11304960 | bytes 1976969 | tf_op jit(solution)/shard_map/while/body/eval_jaxpr/mul | solution.py:104
  470.1 1.6 fusion.55
  476.8 27.5 %fusion.54 = (bf16[8,1,160,384]{3,2,1,0:T(8,128)(2,1)S(1)}, bf16[8,1,160,384]{3,2,1,0:T(8,128)(2,1)S(1)}) fusion(bf16[8,160]{1,0:T(8,128)(2,1)S(1)} %compare_select_fusion.5, pred[8,160]{1,0:T(8,128)(4,1)S(1)} %broadcast_compare_fusion.4, pred[384]{0:T(512)(128)(4,1)S(1)} %compare_and_fusion.2, f32[]{:T(128)S(6)} %convert_element_type.197, ...), kind=kLoop, calls=%fused_computation.17.clone.1 | loop fusion | flops 11304960 | bytes 1976969 | tf_op jit(solution)/shard_map/while/body/eval_jaxpr/mul | solution.py:104
  504.3 1.6 fusion.55
  511.0 27.5 %fusion.54 = (bf16[8,1,160,384]{3,2,1,0:T(8,128)(2,1)S(1)}, bf16[8,1,160,384]{3,2,1,0:T(8,128)(2,1)S(1)}) fusion(bf16[8,160]{1,0:T(8,128)(2,1)S(1)} %compare_select_fusion.5, pred[8,160]{1,0:T(8,128)(4,1)S(1)} %broadcast_compare_fusion.4, pred[384]{0:T(512)(128)(4,1)S(1)} %compare_and_fusion.2, f32[]{:T(128)S(6)} %convert_element_type.197, ...), kind=kLoop, calls=%fused_computation.17.clone.1 | loop fusion | flops 11304960 | bytes 1976969 | tf_op jit(solution)/shard_map/while/body/eval_jaxpr/mul | solution.py:104
  538.5 1.5 fusion.55
  545.1 27.5 %fusion.54 = (bf16[8,1,160,384]{3,2,1,0:T(8,128)(2,1)S(1)}, bf16[8,1,160,384]{3,2,1,0:T(8,128)(2,1)S(1)}) fusion(bf16[8,160]{1,0:T(8,128)(2,1)S(1)} %compare_select_fusion.5, pred[8,160]{1,0:T(8,128)(4,1)S(1)} %broadcast_compare_fusion.4, pred[384]{0:T(512)(128)(4,1)S(1)} %compare_and_fusion.2, f32[]{:T(128)S(6)} %convert_element_type.197, ...), kind=kLoop, calls=%fused_computation.17.clone.1 | loop fusion | flops 11304960 | bytes 1976969 | tf_op jit(solution)/shard_map/while/body/eval_jaxpr/mul | solution.py:104
  572.6 1.5 fusion.55
  579.3 27.5 %fusion.54 = (bf16[8,1,160,384]{3,2,1,0:T(8,128)(2,1)S(1)}, bf16[8,1,160,384]{3,2,1,0:T(8,128)(2,1)S(1)}) fusion(bf16[8,160]{1,0:T(8,128)(2,1)S(1)} %compare_select_fusion.5, pred[8,160]{1,0:T(8,128)(4,1)S(1)} %broadcast_compare_fusion.4, pred[384]{0:T(512)(128)(4,1)S(1)} %compare_and_fusion.2, f32[]{:T(128)S(6)} %convert_element_type.197, ...), kind=kLoop, calls=%fused_computation.17.clone.1 | loop fusion | flops 11304960 | bytes 1976969 | tf_op jit(solution)/shard_map/while/body/eval_jaxpr/mul | solution.py:104
  606.8 1.6 fusion.55
  613.5 27.5 %fusion.54 = (bf16[8,1,160,384]{3,2,1,0:T(8,128)(2,1)S(1)}, bf16[8,1,160,384]{3,2,1,0:T(8,128)(2,1)S(1)}) fusion(bf16[8,160]{1,0:T(8,128)(2,1)S(1)} %compare_select_fusion.5, pred[8,160]{1,0:T(8,128)(4,1)S(1)} %broadcast_compare_fusion.4, pred[384]{0:T(512)(128)(4,1)S(1)} %compare_and_fusion.2, f32[]{:T(128)S(6)} %convert_element_type.197, ...), kind=kLoop, calls=%fused_computation.17.clone.1 | loop fusion | flops 11304960 | bytes 1976969 | tf_op jit(solution)/shard_map/while/body/eval_jaxpr/mul | solution.py:104
  640.9 1.6 fusion.55
  647.6 27.5 %fusion.54 = (bf16[8,1,160,384]{3,2,1,0:T(8,128)(2,1)S(1)}, bf16[8,1,160,384]{3,2,1,0:T(8,128)(2,1)S(1)}) fusion(bf16[8,160]{1,0:T(8,128)(2,1)S(1)} %compare_select_fusion.5, pred[8,160]{1,0:T(8,128)(4,1)S(1)} %broadcast_compare_fusion.4, pred[384]{0:T(512)(128)(4,1)S(1)} %compare_and_fusion.2, f32[]{:T(128)S(6)} %convert_element_type.197, ...), kind=kLoop, calls=%fused_computation.17.clone.1 | loop fusion | flops 11304960 | bytes 1976969 | tf_op jit(solution)/shard_map/while/body/eval_jaxpr/mul | solution.py:104
  675.1 1.6 fusion.55
  681.9 27.5 %fusion.54 = (bf16[8,1,160,384]{3,2,1,0:T(8,128)(2,1)S(1)}, bf16[8,1,160,384]{3,2,1,0:T(8,128)(2,1)S(1)}) fusion(bf16[8,160]{1,0:T(8,128)(2,1)S(1)} %compare_select_fusion.5, pred[8,160]{1,0:T(8,128)(4,1)S(1)} %broadcast_compare_fusion.4, pred[384]{0:T(512)(128)(4,1)S(1)} %compare_and_fusion.2, f32[]{:T(128)S(6)} %convert_element_type.197, ...), kind=kLoop, calls=%fused_computation.17.clone.1 | loop fusion | flops 11304960 | bytes 1976969 | tf_op jit(solution)/shard_map/while/body/eval_jaxpr/mul | solution.py:104
  709.3 1.5 fusion.55
  716.0 27.5 %fusion.54 = (bf16[8,1,160,384]{3,2,1,0:T(8,128)(2,1)S(1)}, bf16[8,1,160,384]{3,2,1,0:T(8,128)(2,1)S(1)}) fusion(bf16[8,160]{1,0:T(8,128)(2,1)S(1)} %compare_select_fusion.5, pred[8,160]{1,0:T(8,128)(4,1)S(1)} %broadcast_compare_fusion.4, pred[384]{0:T(512)(128)(4,1)S(1)} %compare_and_fusion.2, f32[]{:T(128)S(6)} %convert_element_type.197, ...), kind=kLoop, calls=%fused_computation.17.clone.1 | loop fusion | flops 11304960 | bytes 1976969 | tf_op jit(solution)/shard_map/while/body/eval_jaxpr/mul | solution.py:104
  743.5 1.6 fusion.55
  750.2 27.5 %fusion.54 = (bf16[8,1,160,384]{3,2,1,0:T(8,128)(2,1)S(1)}, bf16[8,1,160,384]{3,2,1,0:T(8,128)(2,1)S(1)}) fusion(bf16[8,160]{1,0:T(8,128)(2,1)S(1)} %compare_select_fusion.5, pred[8,160]{1,0:T(8,128)(4,1)S(1)} %broadcast_compare_fusion.4, pred[384]{0:T(512)(128)(4,1)S(1)} %compare_and_fusion.2, f32[]{:T(128)S(6)} %convert_element_type.197, ...), kind=kLoop, calls=%fused_computation.17.clone.1 | loop fusion | flops 11304960 | bytes 1976969 | tf_op jit(solution)/shard_map/while/body/eval_jaxpr/mul | solution.py:104
  777.7 1.5 fusion.55
  779.2 30.5 %fusion.26 = f32[16,96,384]{2,1,0:T(8,128)} fusion(bf16[16,8,2,160,384]{4,3,2,1,0:T(8,128)(2,1)} %get-tuple-element.101, bf16[8,16,2,96,160]{4,1,2,0,3:T(8,128)(2,1)} %all-gather.2.cloned.1.call-done), kind=kOutput, calls=%fused_computation.42 | convolution fusion | flops 3019898880 | bytes 41680896 | tf_op jit(solution)/shard_map/asrgk,sarkx->sgx/dot_general | solution.py:181
  809.7 3.0 reshape.379
  812.7 1.4 copy.70
  814.1 1.4 slice_bitcast_fusion
  (153 shorter events, 57.3 us)
Async XLA Ops:
  7.2 5.0 copy-start.6
  43.9 5.5 copy-start.7
  57.9 3.1 copy-start
  57.9 3.1 copy-start.2
  57.9 3.1 copy-start.3
  61.0 14.3 %copy-start.1 = (bf16[1,2,2,80,1281]{3,1,0,2,4:T(2,128)(2,1)S(1)}, bf16[1,2,2,80,1281]{3,1,0,2,4:T(2,128)(2,1)}, u32[]{:S(2)}) copy-start(bf16[1,2,2,80,1281]{3,1,0,2,4:T(2,128)(2,1)} %copy.55) | copy-start | bytes 2459524
  86.7 16.0 %copy-start.5 = (pred[80,641,2,1]{0,2,1,3:T(4,128)(4,1)S(1)}, pred[80,641,2,1]{0,2,1,3:T(4,128)(4,1)}, u32[]{:S(2)}) copy-start(pred[80,641,2,1]{0,2,1,3:T(4,128)(4,1)} %not.12) | copy-start | bytes 307684
  86.7 16.3 %copy-start.8 = (pred[80,641,2,1]{1,0,3,2:T(8,128)(4,1)S(1)}, pred[80,641,2,1]{1,0,3,2:T(8,128)(4,1)}, u32[]{:S(2)}) copy-start(pred[80,641,2,1]{1,0,3,2:T(8,128)(4,1)} %copy.58) | copy-start | bytes 307684
  200.2 2.5 copy-start.9
  208.6 10.9 %copy-start.10 = (s32[96]{0:T(128)S(1)}, s32[96]{0:T(128)}, u32[]{:S(2)}) copy-start(s32[96]{0:T(128)} %param.14) | copy-start | bytes 1156
  213.7 18.7 %copy-start.4 = (s32[8,160]{1,0:T(8,128)S(1)}, s32[8,160]{1,0:T(8,128)}, u32[]{:S(2)}) copy-start(s32[8,160]{1,0:T(8,128)} %param.13) | copy-start | bytes 15364
  213.7 17.7 %all-to-all-start = ((bf16[8,16,2,6,160]{4,1,3,2,0:T(8,128)(2,1)}), bf16[8,16,2,6,160]{4,1,3,2,0:T(8,128)(2,1)S(1)}, u32[]{:S(2)}, u32[]{:S(2)}) async-start(bf16[8,16,2,6,160]{4,1,3,2,0:T(8,128)(2,1)} %copy.67), calls=%async_computation | async-start | bytes 1572864 | tf_op jit(solution)/shard_map/all_to_all | solution.py:164
  218.2 560.9 %all-gather.2.cloned.1.call-start = ((), (), s32[]{:S(2)}) async-start(), calls=%async_computation.1 | async-start | bytes 13369344 | tf_op jit(solution)/shard_map/all_gather | solution.py:180
Sparse Core Ops, SparseCore 0:
  232.5 90.6 all-gather.1
where the time goes:
time: 835 us; the launch traced here: 823 us
  other arithmetic  530 us (63%)
  local copies, waits for them, and re-layouts  175 us (21%)
  matrix products  45.7 us (5%)
  loops' own time  42.3 us (5%)
  between operations  14.5 us (2%)
  waiting for transfers between devices  10.5 us (1%)
    mul x16, other arithmetic, trig_table(): cosine = jnp.cos(angles).astype(jnp.bfloat16) * weights  440 us
    another operation x1, loops' own time, per_device(): tables = lax.map(one_slot, (lon_counts, occupied))  42.3 us
    reshape x2, local copies, waits for them, and re-layouts, legendre_products(): table = poly_table.reshape(north_count, pair_count, -1)  38.5 us
    dot_general x1, matrix products, per_device(): jnp.einsum('asrgk,sarkx->sgx', gathered, tables, preferred_element_type=j...  30.5 us
    dynamic_update_slice x16, other arithmetic, per_device(): tables = lax.map(one_slot, (lon_counts, occupied))  24.9 us
    mul x1, local copies, waits for them, and re-layouts, legendre_products(): masked_table = table[..., None] * seg_mask[None]  24.4 us
    and x16, other arithmetic, trig_table(): occupied & (longitudes[None, None, :] < lon_count)  20.6 us
    dynamic_slice x32, local copies, waits for them, and re-layouts, per_device(): tables = lax.map(one_slot, (lon_counts, occupied))  19.2 us
  transfers between devices with their start and end apart: 2, of which 1 were waited for; matrix products, arithmetic and copies ran while one was open for 62% of the time, Pallas kernels for 0%

commit v1 on v0

v1 whole, which is shorter than its diff:
```python
import functools
import math

import jax
import jax.numpy as jnp
from jax import lax
from jax.experimental import pallas as pl
from jax.experimental.pallas import tpu as pltpu
from jax.sharding import PartitionSpec as P

MW = 1280
WIDTH = MW + 1
PAIRS = 80
GROUP = 8
STEPS = PAIRS // GROUP
MAIN = GROUP * MW
WIN = 1408
LATH = 48
BAND_MAX = 16
PIECES = 16
PIECE = 384
LEVELS = 32
KM = 64
KR = PAIRS - KM
KALL = 2 * PAIRS
F32 = jnp.float32
BF16 = jnp.bfloat16
NT = (((1,), (1,)), ((), ()))


def wind_legendre_kernel(
    orders,
    limits,
    where_am_i,
    rot,
    rot_x,
    dil,
    dil_x,
    tmp,
    tmp_x,
    pol,
    pol_x,
    out,
    fields,
    heat,
    table,
    coef_a,
    coef_b,
    coef_c,
    north,
    south,
    tiles,
):
    step = pl.program_id(0)
    me = where_am_i[0]
    live = 102480 - (step + 1) * MAIN

    def edge(ref):
        lane = lax.broadcasted_iota(jnp.int32, (2, 128), 1)
        return [jnp.where(lane < live, ref[lv].astype(F32), 0.0).astype(BF16) for lv in range(2)]

    for src, (ref, ref_x) in enumerate(((rot, rot_x), (dil, dil_x))):
        tail = edge(ref_x)
        for lv in range(2):
            row = src * 4 + lv * 2
            fields[row : row + 2, 0:MAIN] = ref[lv]
            fields[row : row + 2, MAIN : MAIN + 128] = tail[lv]
    tail = edge(tmp_x)
    for copy in range(4):
        for lv in range(2):
            row = copy * 4 + lv * 2
            heat[row : row + 2, 0:MAIN] = tmp[lv]
            heat[row : row + 2, MAIN : MAIN + 128] = tail[lv]
    table[:, 0:MAIN] = pol[...]
    lane48 = lax.broadcasted_iota(jnp.int32, (LATH, 128), 1)
    table[:, MAIN : MAIN + 128] = jnp.where(lane48 < live, pol_x[...].astype(F32), 0.0).astype(BF16)

    lane = lax.broadcasted_iota(jnp.int32, (GROUP, WIN), 1)
    sub = lax.broadcasted_iota(jnp.int32, (GROUP, WIN), 0)
    low = [orders[me, 2 * (step * GROUP + s)] for s in range(GROUP)]
    sub1 = lax.broadcasted_iota(jnp.int32, (GROUP, 128), 0)
    lower1 = jnp.zeros((GROUP, 128), jnp.int32)
    for s in range(GROUP):
        lower1 = jnp.where(sub1 == s, low[s], lower1)
    lower = jnp.concatenate([lower1] * (WIN // 128), axis=1)
    pos = lane - sub - step * GROUP
    valid = (pos >= 0) & (pos < WIDTH)
    first = pos < MW - lower
    wave = jnp.where(first, lower, MW - 1 - lower).astype(F32)
    deg = jnp.where(first, lower + pos, pos - 1).astype(F32)
    usable = valid & (deg > 0.5)
    deg = jnp.where(usable, deg, 1.0)
    square = deg * deg
    eps_over_n = jnp.sqrt(
        jnp.maximum((deg - wave) * (deg + wave), 0.0) / ((4.0 * square - 1.0) * square)
    )
    eps_over_n = jnp.where(usable, eps_over_n, 0.0)
    coef_a[...] = jnp.where(deg > 1.5, eps_over_n, 0.0)
    coef_b[...] = pltpu.roll(eps_over_n, WIN - 1, 1)
    coef_c[...] = jnp.where(usable, wave / (square + deg), 0.0)

    early = step < KM // GROUP
    base = jnp.where(early, step * GROUP, 2 * KM + (step - KM // GROUP) * GROUP)
    seg_off = jnp.where(early, KM, KR)

    half_row = lax.broadcasted_iota(jnp.int32, (GROUP, WIN), 0) // 4
    lane_par = lane & 1
    for s in range(GROUP):
        lo = s * MW
        x = fields[:, lo : lo + WIN].astype(F32)
        a = coef_a[pl.ds(s, GROUP, stride=0), :]
        b = coef_b[pl.ds(s, GROUP, stride=0), :]
        c = coef_c[pl.ds(s, GROUP, stride=0), :]
        w = b * pltpu.roll(x, WIN - 1, 1) - a * pltpu.roll(x, 1, 1)
        cx = c * x
        j = step * GROUP + s
        cut = MW - low[s] + j
        in0 = (lane >= j) & (lane < cut)
        in1 = (lane >= cut) & (lane < j + WIDTH)
        par0 = (lane_par ^ (j & 1)) == 0
        par1 = (lane_par ^ ((j + low[s]) & 1)) == 0
        masks = [in0 & par0, in0 & ~par0, in1 & par1, in1 & ~par1]
        rows = []
        for mask in masks:
            rows.append(jnp.where(mask, w, 0.0))
            rows.append(jnp.where(mask, cx, 0.0))
        h = heat[:, lo : lo + WIN].astype(F32)
        top = jnp.where(half_row == 0, masks[0].astype(F32), masks[1].astype(F32))
        bottom = jnp.where(half_row == 0, masks[2].astype(F32), masks[3].astype(F32))
        rows.append(h[0:8] * top)
        rows.append(h[8:16] * bottom)
        data = jnp.concatenate(rows, axis=0).astype(BF16)
        res = lax.dot_general(data, table[:, lo : lo + WIN], NT, preferred_element_type=F32)
        for seg in range(2):
            at = base + s + seg * seg_off
            for part in range(2):
                even = res[seg * 32 + part * 8 : seg * 32 + part * 8 + 8]
                odd = res[seg * 32 + 16 + part * 8 : seg * 32 + 16 + part * 8 + 8]
                north[pl.ds(part * 8 * KALL + at, 8, stride=KALL), :] = even + odd
                south[pl.ds(part * 8 * KALL + at, 8, stride=KALL), :] = even - odd
            both = res[64 + seg * 8 : 72 + seg * 8]
            flip = pltpu.roll(both, 4, 0)
            north[pl.ds(16 * KALL + at, 4, stride=KALL), :] = (both + flip)[0:4]
            south[pl.ds(16 * KALL + at, 4, stride=KALL), :] = (both - flip)[0:4]

    @pl.when(step == STEPS - 1)
    def _():
        dest = lax.broadcasted_iota(jnp.int32, (128, LATH), 0)
        column = lax.broadcasted_iota(jnp.int32, (128, LATH), 1)
        lat = dest % BAND_MAX
        for band in range(8):
            lat = lat + jnp.where(dest // BAND_MAX == band, limits[band], 0)
        pick_n = (lat == column).astype(F32).astype(BF16)
        pick_s = (2 * LATH - 1 - lat == column).astype(F32).astype(BF16)

        def rows_of(ref, part, lv, fld, start, size):
            def at(row):
                return ref[row * KALL + start : row * KALL + start + size, :]

            if fld == 2:
                return at(16 + lv * 2 + part)
            w = at((4 if fld == 1 else 0) + lv * 2 + part)
            cx = at(8 + (0 if fld == 1 else 4) + lv * 2 + 1 - part)
            w = -w if fld == 1 else w
            return w + cx if part == 0 else w - cx

        def select(rows_n, rows_s, row):
            val = lax.dot_general(pick_n, rows_n.astype(BF16), NT, preferred_element_type=F32)
            val = val + lax.dot_general(pick_s, rows_s.astype(BF16), NT, preferred_element_type=F32)
            for block in range(16):
                tiles[pl.ds(row + 128 * block, 8, stride=16), :] = val[8 * block : 8 * block + 8]

        for part in range(2):
            for lv in range(2):
                for fld in range(3):
                    select(
                        rows_of(north, part, lv, fld, 0, 2 * KM),
                        rows_of(south, part, lv, fld, 0, 2 * KM),
                        part * 6 + lv * 3 + fld,
                    )
        for fld in range(3):
            both = []
            for ref in (north, south):
                both.append(
                    jnp.concatenate(
                        [
                            rows_of(ref, q // 2, q % 2, fld, 2 * KM, 2 * KR)
                            for q in range(4)
                        ],
                        axis=0,
                    )
                )
            select(both[0], both[1], 12 + fld)
        for block in range(16):
            tiles[pl.ds(15 + 128 * block, 8, stride=16), :] = jnp.zeros((8, 128), F32)
        for block in range(16):
            part = tiles[128 * block : 128 * block + 128, :]
            out[8 * block : 8 * block + 8] = part.reshape(8, 16, 128).astype(BF16)


def wind_legendre(rot, dil, tmp, pol, orders, limits, me):
    def smem(shape):
        return pl.BlockSpec(shape, lambda i: (0,) * len(shape), memory_space=pltpu.SMEM)

    main = pl.BlockSpec((2, 2, MAIN), lambda i: (0, 0, i))
    tail = pl.BlockSpec((2, 2, 128), lambda i: (0, 0, (i + 1) * (MAIN // 128)))
    return pl.pallas_call(
        wind_legendre_kernel,
        grid=(STEPS,),
        in_specs=[
            smem((8, 160)),
            smem((9,)),
            smem((1,)),
            main,
            tail,
            main,
            tail,
            main,
            tail,
            pl.BlockSpec((LATH, MAIN), lambda i: (0, i)),
            pl.BlockSpec((LATH, 128), lambda i: (0, (i + 1) * (MAIN // 128))),
        ],
        out_specs=pl.BlockSpec((128, 16, 128), lambda i: (0, 0, 0)),
        out_shape=jax.ShapeDtypeStruct((128, 16, 128), BF16),
        scratch_shapes=[
            pltpu.VMEM((8, MAIN + 128), BF16),
            pltpu.VMEM((16, MAIN + 128), BF16),
            pltpu.VMEM((LATH, MAIN + 128), BF16),
            pltpu.VMEM((GROUP, WIN), F32),
            pltpu.VMEM((GROUP, WIN), F32),
            pltpu.VMEM((GROUP, WIN), F32),
            pltpu.VMEM((20 * KALL, LATH), F32),
            pltpu.VMEM((20 * KALL, LATH), F32),
            pltpu.VMEM((2048, 128), F32),
        ],
        compiler_params=pltpu.CompilerParams(vmem_limit_bytes=40 * 1024 * 1024),
        name="wind_legendre",
    )(orders, limits, me, rot, rot, dil, dil, tmp, tmp, pol, pol)


def cos_sin_turns(turns):
    z = turns * (math.pi / 2.0)
    y = z * z
    sin = z * (1.0 + y * (-1 / 6 + y * (1 / 120 + y * (-1 / 5040 + y * (1 / 362880)))))
    cos = 1.0 + y * (-1 / 2 + y * (1 / 24 + y * (-1 / 720 + y * (1 / 40320 + y * (-1 / 3628800)))))
    s2 = 2.0 * sin * cos
    c2 = 1.0 - 2.0 * sin * sin
    return 1.0 - 2.0 * s2 * s2, 2.0 * s2 * c2


def fraction_of_turn(product, count, inverse):
    r = product - jnp.floor(product * inverse + 0.5) * count
    return r * inverse


def table_kernel(count, wave, table, twist_c, twist_s, weight):
    k = count[0].astype(F32)
    k_lane = jnp.maximum(jnp.full((8, 128), k, F32), 1.0)
    inverse = 1.0 / k_lane
    k1, inv1 = k_lane[0:1, 0:1], inverse[0:1, 0:1]
    m_row = wave[...].astype(F32)
    for q in range(2):
        piece = (lax.broadcasted_iota(jnp.int32, (8, MW), 0) + 8 * q).astype(F32)
        cos, sin = cos_sin_turns(fraction_of_turn(piece * m_row, k1, inv1))
        for row in range(8):
            twist_c[8 * q + row] = cos[row : row + 1]
            twist_s[8 * q + row] = sin[row : row + 1]
    top = jnp.full((8, MW), (count[0] - 1) // 2, jnp.int32)
    m8 = jnp.broadcast_to(wave[...], (8, MW))
    w = jnp.where(m8 == 0, 1.0, 2.0)
    weight[...] = jnp.where(m8 <= top, w, 0.0)
    for q in range(MW // 128):
        chunk = jnp.broadcast_to(m_row[:, 128 * q : 128 * q + 128], (128, 128))
        column = jnp.transpose(chunk, (1, 0))
        for c in range(PIECE // 128):
            x = ((lax.broadcasted_iota(jnp.int32, (128, 128), 1) + 128 * c) * PIECES).astype(F32)
            cos, sin = cos_sin_turns(fraction_of_turn(x * column, k1, inv1))
            table[128 * q : 128 * q + 128, 128 * c : 128 * c + 128] = cos.astype(BF16)
            table[MW + 128 * q : MW + 128 * q + 128, 128 * c : 128 * c + 128] = (-sin).astype(BF16)


def make_table(count, wave):
    return pl.pallas_call(
        table_kernel,
        in_specs=[pl.BlockSpec(memory_space=pltpu.SMEM), pl.BlockSpec(memory_space=pltpu.VMEM)],
        out_specs=[pl.BlockSpec(memory_space=pltpu.VMEM)] * 4,
        out_shape=[
            jax.ShapeDtypeStruct((2 * MW, PIECE), BF16),
            jax.ShapeDtypeStruct((PIECES, 1, MW), F32),
            jax.ShapeDtypeStruct((PIECES, 1, MW), F32),
            jax.ShapeDtypeStruct((8, MW), F32),
        ],
        compiler_params=pltpu.CompilerParams(vmem_limit_bytes=32 * 1024 * 1024),
        cost_estimate=pl.CostEstimate(flops=50_000_000, transcendentals=0, bytes_accessed=4_000_000),
        name="trig_table",
    )(count, wave)


PSTEP = 4


def grid_kernel(count, data, table, twist_c, twist_s, weight, out, f_re, f_im, twisted):
    step = pl.program_id(0)

    @pl.when(step == 0)
    def _():
        row = lax.broadcasted_iota(jnp.int32, (192, 256), 0)
        col = lax.broadcasted_iota(jnp.int32, (192, 256), 1)
        pick_main = (col == (row % 16) * 16 + row // 16).astype(F32).astype(BF16)
        pick_rest = (col == (row % 16) * 16 + 12 + (row // 16) % 3).astype(F32).astype(BF16)
        lane = lax.broadcasted_iota(jnp.int32, (48, 128), 1) // 32
        rest = [[jnp.zeros((48, 128), F32) for _ in range(2)] for _ in range(4)]
        for a in range(8):
            x = data[16 * a : 16 * a + 16].reshape(256, 128)
            lanes = slice(128 * a, 128 * a + 128)
            w = weight[0:1, lanes]
            main = jnp.dot(pick_main, x, preferred_element_type=F32)
            f_re[:, lanes] = main[0:96] * w
            f_im[:, lanes] = main[96:192] * w
            more = jnp.dot(pick_rest, x, preferred_element_type=F32)
            for q in range(4):
                piece = more[48 * q : 48 * q + 48]
                shift = (32 * (a % 4) - 32 * q) % 128
                if shift:
                    piece = pltpu.roll(piece, shift, 1)
                rest[q][a // 4] = jnp.where(lane == a % 4, piece, rest[q][a // 4])
        for half in range(2):
            lanes = slice(1024 + 128 * half, 1152 + 128 * half)
            w = weight[0:1, lanes]
            f_re[0:48, lanes] = rest[0][half] * w
            f_re[48:96, lanes] = rest[1][half] * w
            f_im[0:48, lanes] = rest[2][half] * w
            f_im[48:96, lanes] = rest[3][half] * w

    for u in range(PSTEP):
        piece = step * PSTEP + u
        for chunk in range(MW // 128):
            lanes = slice(128 * chunk, 128 * chunk + 128)
            cos = twist_c[piece, :, lanes]
            sin = twist_s[piece, :, lanes]
            re, im = f_re[:, lanes], f_im[:, lanes]
            twisted[96 * u : 96 * u + 96, lanes] = (re * cos - im * sin).astype(BF16)
            twisted[96 * u : 96 * u + 96, MW + 128 * chunk : MW + 128 * chunk + 128] = (
                re * sin + im * cos
            ).astype(BF16)
    res = jnp.dot(twisted[...], table[...], preferred_element_type=F32)
    lon = lax.broadcasted_iota(jnp.int32, (96, PIECE), 1) * PIECES + step * PSTEP
    for u in range(PSTEP):
        keep = lon + u < count[0]
        out[u] = jnp.where(keep, res[96 * u : 96 * u + 96], 0.0).astype(BF16)


def make_grid(count, data, tables):
    def whole(shape):
        return pl.BlockSpec(shape, lambda i: (0,) * len(shape))

    return pl.pallas_call(
        grid_kernel,
        grid=(PIECES // PSTEP,),
        in_specs=[
            pl.BlockSpec((1,), lambda i: (0,), memory_space=pltpu.SMEM),
            whole((128, 16, 128)),
            whole((2 * MW, PIECE)),
            whole((PIECES, 1, MW)),
            whole((PIECES, 1, MW)),
            whole((8, MW)),
        ],
        out_specs=pl.BlockSpec((PSTEP, 96, PIECE), lambda i: (i, 0, 0)),
        out_shape=jax.ShapeDtypeStruct((PIECES, 96, PIECE), BF16),
        scratch_shapes=[
            pltpu.VMEM((96, MW), F32),
            pltpu.VMEM((96, MW), F32),
            pltpu.VMEM((96 * PSTEP, 2 * MW), BF16),
        ],
        compiler_params=pltpu.CompilerParams(vmem_limit_bytes=48 * 1024 * 1024),
        name="grid_product",
    )(count, data, *tables)


def wave_row(orders):
    lower = orders[:, 0::2]
    both = jnp.stack([lower, MW - 1 - lower], axis=1)
    return jnp.concatenate([both[:, :, :KM].reshape(1, -1), both[:, :, KM:].reshape(1, -1)], axis=1)


def per_device(rot, dil, tmp, pol, orders, counts, limits):
    band = lax.axis_index("aa").astype(jnp.int32)
    slot = lax.axis_index("ba").astype(jnp.int32)
    sent = wind_legendre(rot, dil, tmp, pol, orders, limits, band[None])
    got = lax.all_to_all(sent, ("aa", "ba"), split_axis=0, concat_axis=0, tiled=True)
    edges = lax.dynamic_slice_in_dim(limits, band, 2, 0)
    lat = edges[0] + slot
    count = jnp.where(lat < edges[1], jnp.sum(jnp.where(jnp.arange(96) == lat, counts, 0)), 0)
    count = count.astype(jnp.int32)[None]
    tables = make_table(count, wave_row(orders))
    pieces = make_grid(count, got, tables)
    rows = lax.all_to_all(pieces, "ba", split_axis=0, concat_axis=0, tiled=True)
    rows = rows.reshape(BAND_MAX, 2, 3, PIECES, PIECE).astype(F32)
    outs = jnp.transpose(rows, (2, 3, 1, 0, 4)).reshape(3, LEVELS, BAND_MAX, PIECE)
    return outs[0], outs[1], outs[2]


def solution(mesh):
    return jax.shard_map(
        per_device,
        mesh=mesh,
        in_specs=(
            P("ba", None, "aa"),
            P("ba", None, "aa"),
            P("ba", None, "aa"),
            P(None, "aa"),
            P(),
            P(),
            P(),
        ),
        out_specs=(P(None, "aa", "ba"), P(None, "aa", "ba"), P(None, "aa", "ba")),
        check_vma=False,
    )
```

time: 835 us -> 85.8 us (0.10); the launches traced: 823 us -> 85.4 us
  other arithmetic: 530 us -> 0.99 us
  local copies, waits for them, and re-layouts: 175 us -> 13.9 us
  matrix products: 45.7 us -> 0 us
  loops' own time: 42.3 us -> 0 us
  Pallas kernels: 0 us -> 28.3 us
  blocking collectives: 0 us -> 21.3 us
  between operations: 14.5 us -> 2.69 us
    mul x18 -> x0, other arithmetic: 442 us -> none  [the longest x16 440 us: trig_table(): cosine = jnp.cos(angles).astype(jnp.bfloat16) * weights]
    reshape x5 -> x2, local copies, waits for them, and re-layouts: 62.5 us -> 0.18 us  [the longest x1 0.09 us: wave_row(): both[:, :, KM:].reshape(1, -1)]
    dot_general x2 -> x0, matrix products: 45.7 us -> none  [the longest x1 30.5 us: per_device(): jnp.einsum('asrgk,sarkx->sgx', gathered, tables, preferred_element_type=j...]
    another operation x1 -> x0, loops' own time: 42.3 us -> none  [per_device(): tables = lax.map(one_slot, (lon_counts, occupied))]
    pallas_call x0 -> x3, Pallas kernels: none -> 28.3 us  [the longest x1 20 us: wind_legendre(): pl.pallas_call(wind_legendre_kernel, grid=(STEPS,), in_specs=[smem((8, 16...]
    dynamic_update_slice x16 -> x0, other arithmetic: 24.9 us -> none  [per_device(): tables = lax.map(one_slot, (lon_counts, occupied))]
    mul x1 -> x0, local copies, waits for them, and re-layouts: 24.4 us -> none  [legendre_products(): masked_table = table[..., None] * seg_mask[None]]
    all_to_all x0 -> x1, blocking collectives: none -> 21.3 us  [per_device(): rows = lax.all_to_all(pieces, 'ba', split_axis=0, concat_axis=0, tiled=True)]
  transfers between devices with their start and end apart: 2 -> 1, of which waited for: 1 -> 1; matrix products, arithmetic and copies ran while one was open for 62% -> 2% of each run, Pallas kernels for 0% -> 3%
where the time goes in v1:
time: 85.8 us; the launch traced here: 85.4 us
  Pallas kernels  28.3 us (33%)
  blocking collectives  21.3 us (25%)
  local copies, waits for them, and re-layouts  13.9 us (16%)
  starting transfers between devices  11.1 us (13%)
  waiting for transfers between devices  7.05 us (8%)
  between operations  2.69 us (3%)
  other arithmetic  0.99 us (1%)
    all_to_all x1, blocking collectives, per_device(): rows = lax.all_to_all(pieces, 'ba', split_axis=0, concat_axis=0, tiled=True)  21.3 us
    pallas_call x1, Pallas kernels, wind_legendre(): pl.pallas_call(wind_legendre_kernel, grid=(STEPS,), in_specs=[smem((8, 16...  20 us
    all_to_all x1, starting transfers between devices, per_device(): lax.all_to_all(sent, ('aa', 'ba'), split_axis=0, concat_axis=0, tiled=True)  11.1 us
    unnamed x18, local copies, waits for them, and re-layouts  8.58 us
    all_to_all x1, waiting for transfers between devices, per_device(): lax.all_to_all(sent, ('aa', 'ba'), split_axis=0, concat_axis=0, tiled=True)  7.05 us
    pallas_call x1, Pallas kernels, make_grid(): pl.pallas_call(grid_kernel, grid=(PIECES // PSTEP,), in_specs=[pl.BlockSp...  5.44 us
    slice x4, local copies, waits for them, and re-layouts, per_device(): return (outs[0], outs[1], outs[2])  4.31 us
    pallas_call x1, Pallas kernels, make_table(): pl.pallas_call(table_kernel, in_specs=[pl.BlockSpec(memory_space=pltpu.SM...  2.82 us
  transfers between devices with their start and end apart: 1, of which 1 were waited for; matrix products, arithmetic and copies ran while one was open for 2% of the time, Pallas kernels for 3%

profile of v1, /device:TPU:0, one launch (start us, length us, event | category | flops | bytes accessed | tf_op | source)
XLA Modules:
  0.0 85.4 jit_solution(1915436302687761560)
XLA Ops:
  0.6 0.0 copy-start
  0.6 3.8 %copy-done = bf16[48,102480]{1,0:T(8,128)(2,1)S(1)} copy-done((bf16[48,102480]{1,0:T(8,128)(2,1)S(1)}, bf16[48,102480]{1,0:T(8,128)(2,1)}, u32[]{:S(2)}) %copy-start) | copy-done | bytes 9838104
  4.4 0.0 copy-start.1
  4.4 1.1 %copy-done.1 = bf16[2,2,102480]{2,1,0:T(2,128)(2,1)S(1)} copy-done((bf16[2,2,102480]{2,1,0:T(2,128)(2,1)S(1)}, bf16[2,2,102480]{2,1,0:T(2,128)(2,1)}, u32[]{:S(2)}) %copy-start.1) | copy-done | bytes 819864
  5.6 0.0 copy-start.2
  5.6 1.1 %copy-done.2 = bf16[2,2,102480]{2,1,0:T(2,128)(2,1)S(1)} copy-done((bf16[2,2,102480]{2,1,0:T(2,128)(2,1)S(1)}, bf16[2,2,102480]{2,1,0:T(2,128)(2,1)}, u32[]{:S(2)}) %copy-start.2) | copy-done | bytes 819864
  6.7 0.0 copy-start.3
  6.7 1.1 %copy-done.3 = bf16[2,2,102480]{2,1,0:T(2,128)(2,1)S(1)} copy-done((bf16[2,2,102480]{2,1,0:T(2,128)(2,1)S(1)}, bf16[2,2,102480]{2,1,0:T(2,128)(2,1)}, u32[]{:S(2)}) %copy-start.3) | copy-done | bytes 819864
  7.9 0.0 copy-start.4
  7.9 0.7 copy-done.4
  8.6 0.0 copy-start.6
  8.6 0.7 copy-done.6
  9.2 0.0 copy-start.5
  9.2 0.0 copy-start.7
  9.2 0.0 copy-start.8
  9.2 20.0 %wind_legendre.1 = bf16[128,16,128]{2,1,0:T(8,128)(2,1)} custom-call(s32[8,160]{1,0:T(8,128)S(1)} %copy-done.4, s32[9]{0:T(128)S(1)} %copy-done.6, s32[1]{0:T(128)} %bitcast.3.where_am_i, bf16[2,2,102480]{2,1,0:T(2,128)(2,1)S(1)} %copy-done.1, bf16[2,2,102480]{2,1,0:T(2,128)(2,1)S(1)} %copy-done.1, bf16[2,2,102480]{2,1,0:T(2,128)(2,1)S(1)} %copy-done.2, ...), custom_call_target="tpu_custom_call" | custom-call | tf_op jit(solution)/shard_map/wind_legendre/pallas_call | solution.py:207
  29.3 11.1 %all-to-all-start = ((bf16[128,16,128]{2,1,0:T(8,128)(2,1)}), bf16[128,16,128]{2,1,0:T(8,128)(2,1)S(1)}, u32[]{:S(2)}, u32[]{:S(2)}) async-start(bf16[128,16,128]{2,1,0:T(8,128)(2,1)} %wind_legendre.1), calls=%async_computation | async-start | bytes 1048576 | tf_op jit(solution)/shard_map/all_to_all | solution.py:390
  40.4 0.0 copy-done.5
  40.4 0.2 slice.29
  40.6 0.0 copy-done.7
  40.6 0.1 dynamic_slice.3
  40.7 0.1 reshape.22
  40.8 0.1 pad_add_fusion
  40.9 0.1 reshape.23
  41.0 0.6 fusion.2
  42.8 0.0 copy-done.8
  42.9 0.6 fusion
  44.1 2.8 %trig_table.1 = (bf16[2560,384]{1,0:T(8,128)(2,1)S(1)}, f32[16,1,1280]{2,1,0:T(1,128)S(1)}, f32[16,1,1280]{2,1,0:T(1,128)S(1)}, f32[8,1280]{1,0:T(8,128)S(1)}) custom-call(s32[1]{0:T(128)} %bitcast.2.count, s32[1,1280]{1,0:T(1,128)S(1)} %pad_add_fusion.1.wave), custom_call_target="tpu_custom_call" | custom-call | flops 50000000 | bytes 4000000 | tf_op jit(solution)/shard_map/trig_table/pallas_call | solution.py:283
  47.0 7.0 %all-to-all-done.data = bf16[128,16,128]{2,1,0:T(8,128)(2,1)S(1)} async-done(((bf16[128,16,128]{2,1,0:T(8,128)(2,1)}), bf16[128,16,128]{2,1,0:T(8,128)(2,1)S(1)}, u32[]{:S(2)}, u32[]{:S(2)}) %all-to-all-start) | async-done | bytes 524320 | tf_op jit(solution)/shard_map/all_to_all | solution.py:390
  54.0 5.4 %grid_product.1 = bf16[16,96,384]{2,1,0:T(8,128)(2,1)S(1)} custom-call(s32[1]{0:T(128)} %bitcast.2.count, bf16[128,16,128]{2,1,0:T(8,128)(2,1)S(1)} %all-to-all-done.data, bf16[2560,384]{1,0:T(8,128)(2,1)S(1)} %get-tuple-element.7.table, f32[16,1,1280]{2,1,0:T(1,128)S(1)} %get-tuple-element.8.twist_c, f32[16,1,1280]{2,1,0:T(1,128)S(1)} %get-tuple-element.9.twist_s, ...), custom_call_target="tpu_custom_call" | custom-call | tf_op jit(solution)/shard_map/grid_product/pallas_call | solution.py:357
  59.5 21.3 %all_to_all.10 = bf16[16,96,384]{2,1,0:T(8,128)(2,1)S(1)} all-to-all(bf16[16,96,384]{2,1,0:T(8,128)(2,1)S(1)} %grid_product.1), channel_id=1, replica_groups=mesh['aa'=8,'ba'=16] {'ba'}, dimensions={0} | all-to-all | bytes 2359296 | tf_op jit(solution)/shard_map/all_to_all | solution.py:397
  80.8 0.3 convert_bitcast_fusion
  81.0 0.3 fusion.1
  81.3 1.3 %copy.14 = f32[1,16,2,16,384]{4,3,2,1,0:T(8,128)} copy(f32[1,16,2,16,384]{4,1,0,2,3:T(8,128)S(1)} %get-tuple-element.11) | data formatting | bytes 1572864 | tf_op jit(solution)/shard_map/slice | solution.py:400
  82.7 1.3 %copy.13 = f32[1,16,2,16,384]{4,3,2,1,0:T(8,128)} copy(f32[1,16,2,16,384]{4,1,0,2,3:T(8,128)S(1)} %get-tuple-element.12) | data formatting | bytes 1572864 | tf_op jit(solution)/shard_map/slice | solution.py:400
  84.0 1.3 %copy.12 = f32[1,16,2,16,384]{4,3,2,1,0:T(8,128)} copy(f32[1,16,2,16,384]{4,1,0,2,3:T(8,128)S(1)} %get-tuple-element.13) | data formatting | bytes 1572864 | tf_op jit(solution)/shard_map/slice | solution.py:400
  (5 shorter events, 0.0 us)
Async XLA Ops:
  0.6 3.8 %copy-start = (bf16[48,102480]{1,0:T(8,128)(2,1)S(1)}, bf16[48,102480]{1,0:T(8,128)(2,1)}, u32[]{:S(2)}) copy-start(bf16[48,102480]{1,0:T(8,128)(2,1)} %pol_x.1) | copy-start | bytes 29514244
  4.4 1.1 %copy-start.1 = (bf16[2,2,102480]{2,1,0:T(2,128)(2,1)S(1)}, bf16[2,2,102480]{2,1,0:T(2,128)(2,1)}, u32[]{:S(2)}) copy-start(bf16[2,2,102480]{2,1,0:T(2,128)(2,1)} %rot_x.1) | copy-start | bytes 2459524
  5.6 1.1 %copy-start.2 = (bf16[2,2,102480]{2,1,0:T(2,128)(2,1)S(1)}, bf16[2,2,102480]{2,1,0:T(2,128)(2,1)}, u32[]{:S(2)}) copy-start(bf16[2,2,102480]{2,1,0:T(2,128)(2,1)} %dil_x.1) | copy-start | bytes 2459524
  6.7 1.1 %copy-start.3 = (bf16[2,2,102480]{2,1,0:T(2,128)(2,1)S(1)}, bf16[2,2,102480]{2,1,0:T(2,128)(2,1)}, u32[]{:S(2)}) copy-start(bf16[2,2,102480]{2,1,0:T(2,128)(2,1)} %tmp_x.1) | copy-start | bytes 2459524
  7.9 0.7 copy-start.4
  8.6 0.7 copy-start.6
  9.2 31.2 %copy-start.5 = (s32[8,160]{1,0:T(8,128)S(1)}, s32[8,160]{1,0:T(8,128)}, u32[]{:S(2)}) copy-start(s32[8,160]{1,0:T(8,128)} %orders.1) | copy-start | bytes 15364
  9.2 31.4 %copy-start.7 = (s32[9]{0:T(128)S(1)}, s32[9]{0:T(128)}, u32[]{:S(2)}) copy-start(s32[9]{0:T(128)} %limits.1) | copy-start | bytes 112
  9.2 33.6 %copy-start.8 = (s32[96]{0:T(128)S(1)}, s32[96]{0:T(128)}, u32[]{:S(2)}) copy-start(s32[96]{0:T(128)} %param.12) | copy-start | bytes 1156
  29.3 24.8 %all-to-all-start = ((bf16[128,16,128]{2,1,0:T(8,128)(2,1)}), bf16[128,16,128]{2,1,0:T(8,128)(2,1)S(1)}, u32[]{:S(2)}, u32[]{:S(2)}) async-start(bf16[128,16,128]{2,1,0:T(8,128)(2,1)} %wind_legendre.1), calls=%async_computation | async-start | bytes 1048576 | tf_op jit(solution)/shard_map/all_to_all | solution.py:390

commit v2 on v1

--- a/solution.py
+++ b/solution.py
@@ -42,11 +42,11 @@
     pol_x,
     out,
     fields,
-    heat,
-    table,
+    last,
     coef_a,
     coef_b,
     coef_c,
+    masks,
     north,
     south,
     tiles,
@@ -55,25 +55,18 @@
     me = where_am_i[0]
     live = 102480 - (step + 1) * MAIN
 
-    def edge(ref):
-        lane = lax.broadcasted_iota(jnp.int32, (2, 128), 1)
-        return [jnp.where(lane < live, ref[lv].astype(F32), 0.0).astype(BF16) for lv in range(2)]
-
-    for src, (ref, ref_x) in enumerate(((rot, rot_x), (dil, dil_x))):
-        tail = edge(ref_x)
+    def edge(ref, lv):
+        lane2 = lax.broadcasted_iota(jnp.int32, (2, 128), 1)
+        return jnp.where(lane2 < live, ref[lv].astype(F32), 0.0).astype(BF16)
+
+    for src, (ref, ref_x) in enumerate(((rot, rot_x), (dil, dil_x), (tmp, tmp_x), (tmp, tmp_x))):
         for lv in range(2):
             row = src * 4 + lv * 2
             fields[row : row + 2, 0:MAIN] = ref[lv]
-            fields[row : row + 2, MAIN : MAIN + 128] = tail[lv]
-    tail = edge(tmp_x)
-    for copy in range(4):
-        for lv in range(2):
-            row = copy * 4 + lv * 2
-            heat[row : row + 2, 0:MAIN] = tmp[lv]
-            heat[row : row + 2, MAIN : MAIN + 128] = tail[lv]
-    table[:, 0:MAIN] = pol[...]
+            fields[row : row + 2, MAIN : MAIN + 128] = edge(ref_x, lv)
+    last[:, 0:MW] = pol[:, MAIN - MW : MAIN]
     lane48 = lax.broadcasted_iota(jnp.int32, (LATH, 128), 1)
-    table[:, MAIN : MAIN + 128] = jnp.where(lane48 < live, pol_x[...].astype(F32), 0.0).astype(BF16)
+    last[:, MW:WIN] = jnp.where(lane48 < live, pol_x[...].astype(F32), 0.0).astype(BF16)
 
     lane = lax.broadcasted_iota(jnp.int32, (GROUP, WIN), 1)
     sub = lax.broadcasted_iota(jnp.int32, (GROUP, WIN), 0)
@@ -86,10 +79,16 @@
     pos = lane - sub - step * GROUP
     valid = (pos >= 0) & (pos < WIDTH)
     first = pos < MW - lower
-    wave = jnp.where(first, lower, MW - 1 - lower).astype(F32)
-    deg = jnp.where(first, lower + pos, pos - 1).astype(F32)
-    usable = valid & (deg > 0.5)
-    deg = jnp.where(usable, deg, 1.0)
+    wave_i = jnp.where(first, lower, MW - 1 - lower)
+    deg_i = jnp.where(first, lower + pos, pos - 1)
+    even = ((deg_i - wave_i) & 1) == 0
+    masks[0] = jnp.where(valid & first & even, 1.0, 0.0)
+    masks[1] = jnp.where(valid & first & ~even, 1.0, 0.0)
+    masks[2] = jnp.where(valid & ~first & even, 1.0, 0.0)
+    masks[3] = jnp.where(valid & ~first & ~even, 1.0, 0.0)
+    wave = wave_i.astype(F32)
+    usable = valid & (deg_i > 0)
+    deg = jnp.where(usable, deg_i, 1).astype(F32)
     square = deg * deg
     eps_over_n = jnp.sqrt(
         jnp.maximum((deg - wave) * (deg + wave), 0.0) / ((4.0 * square - 1.0) * square)
@@ -103,45 +102,41 @@
     base = jnp.where(early, step * GROUP, 2 * KM + (step - KM // GROUP) * GROUP)
     seg_off = jnp.where(early, KM, KR)
 
-    half_row = lax.broadcasted_iota(jnp.int32, (GROUP, WIN), 0) // 4
-    lane_par = lane & 1
+    row8 = lax.broadcasted_iota(jnp.int32, (8, WIN), 0)
+    row_even = (row8 & 1) == 0
+    top_half = row8 < 4
+    sign = jnp.where(row_even == top_half, 1.0, -1.0)
+
+    def spread(ref, s):
+        return ref[pl.ds(s, 8, stride=0), :]
+
     for s in range(GROUP):
         lo = s * MW
-        x = fields[:, lo : lo + WIN].astype(F32)
-        a = coef_a[pl.ds(s, GROUP, stride=0), :]
-        b = coef_b[pl.ds(s, GROUP, stride=0), :]
-        c = coef_c[pl.ds(s, GROUP, stride=0), :]
-        w = b * pltpu.roll(x, WIN - 1, 1) - a * pltpu.roll(x, 1, 1)
-        cx = c * x
-        j = step * GROUP + s
-        cut = MW - low[s] + j
-        in0 = (lane >= j) & (lane < cut)
-        in1 = (lane >= cut) & (lane < j + WIDTH)
-        par0 = (lane_par ^ (j & 1)) == 0
-        par1 = (lane_par ^ ((j + low[s]) & 1)) == 0
-        masks = [in0 & par0, in0 & ~par0, in1 & par1, in1 & ~par1]
-        rows = []
-        for mask in masks:
-            rows.append(jnp.where(mask, w, 0.0))
-            rows.append(jnp.where(mask, cx, 0.0))
-        h = heat[:, lo : lo + WIN].astype(F32)
-        top = jnp.where(half_row == 0, masks[0].astype(F32), masks[1].astype(F32))
-        bottom = jnp.where(half_row == 0, masks[2].astype(F32), masks[3].astype(F32))
-        rows.append(h[0:8] * top)
-        rows.append(h[8:16] * bottom)
+        both = fields[:, lo : lo + WIN].astype(F32)
+        x, heat = both[0:8], both[8:16]
+        other = jnp.where(row_even, pltpu.roll(x, 3, 0), pltpu.roll(x, 5, 0))
+        wind = (
+            spread(coef_b, s) * pltpu.roll(x, WIN - 1, 1)
+            - spread(coef_a, s) * pltpu.roll(x, 1, 1)
+            + spread(coef_c, s) * (other * sign)
+        )
+        m = [spread(masks.at[g], s) for g in range(4)]
+        rows = [wind * m[g] for g in range(4)]
+        rows.append(heat * jnp.where(top_half, m[0], m[1]))
+        rows.append(heat * jnp.where(top_half, m[2], m[3]))
         data = jnp.concatenate(rows, axis=0).astype(BF16)
-        res = lax.dot_general(data, table[:, lo : lo + WIN], NT, preferred_element_type=F32)
+        poly = last[...] if s == GROUP - 1 else pol[:, lo : lo + WIN]
+        res = lax.dot_general(data, poly, NT, preferred_element_type=F32)
         for seg in range(2):
             at = base + s + seg * seg_off
-            for part in range(2):
-                even = res[seg * 32 + part * 8 : seg * 32 + part * 8 + 8]
-                odd = res[seg * 32 + 16 + part * 8 : seg * 32 + 16 + part * 8 + 8]
-                north[pl.ds(part * 8 * KALL + at, 8, stride=KALL), :] = even + odd
-                south[pl.ds(part * 8 * KALL + at, 8, stride=KALL), :] = even - odd
-            both = res[64 + seg * 8 : 72 + seg * 8]
-            flip = pltpu.roll(both, 4, 0)
-            north[pl.ds(16 * KALL + at, 4, stride=KALL), :] = (both + flip)[0:4]
-            south[pl.ds(16 * KALL + at, 4, stride=KALL), :] = (both - flip)[0:4]
+            plus = res[seg * 16 : seg * 16 + 8]
+            minus = res[seg * 16 + 8 : seg * 16 + 16]
+            north[pl.ds(at, 8, stride=KALL), :] = plus + minus
+            south[pl.ds(at, 8, stride=KALL), :] = plus - minus
+            pair = res[32 + seg * 8 : 40 + seg * 8]
+            flip = pltpu.roll(pair, 4, 0)
+            north[pl.ds(8 * KALL + at, 4, stride=KALL), :] = (pair + flip)[0:4]
+            south[pl.ds(8 * KALL + at, 4, stride=KALL), :] = (pair - flip)[0:4]
 
     @pl.when(step == STEPS - 1)
     def _():
@@ -154,19 +149,13 @@
         pick_s = (2 * LATH - 1 - lat == column).astype(F32).astype(BF16)
 
         def rows_of(ref, part, lv, fld, start, size):
-            def at(row):
-                return ref[row * KALL + start : row * KALL + start + size, :]
-
-            if fld == 2:
-                return at(16 + lv * 2 + part)
-            w = at((4 if fld == 1 else 0) + lv * 2 + part)
-            cx = at(8 + (0 if fld == 1 else 4) + lv * 2 + 1 - part)
-            w = -w if fld == 1 else w
-            return w + cx if part == 0 else w - cx
+            row = fld * 4 + lv * 2 + part
+            val = ref[row * KALL + start : row * KALL + start + size, :]
+            return (-val if fld == 1 else val).astype(BF16)
 
         def select(rows_n, rows_s, row):
-            val = lax.dot_general(pick_n, rows_n.astype(BF16), NT, preferred_element_type=F32)
-            val = val + lax.dot_general(pick_s, rows_s.astype(BF16), NT, preferred_element_type=F32)
+            val = lax.dot_general(pick_n, rows_n, NT, preferred_element_type=F32)
+            val = val + lax.dot_general(pick_s, rows_s, NT, preferred_element_type=F32)
             for block in range(16):
                 tiles[pl.ds(row + 128 * block, 8, stride=16), :] = val[8 * block : 8 * block + 8]
 
@@ -183,10 +172,7 @@
             for ref in (north, south):
                 both.append(
                     jnp.concatenate(
-                        [
-                            rows_of(ref, q // 2, q % 2, fld, 2 * KM, 2 * KR)
-                            for q in range(4)
-                        ],
+                        [rows_of(ref, q // 2, q % 2, fld, 2 * KM, 2 * KR) for q in range(4)],
                         axis=0,
                     )
                 )
@@ -204,6 +190,9 @@
 
     main = pl.BlockSpec((2, 2, MAIN), lambda i: (0, 0, i))
     tail = pl.BlockSpec((2, 2, 128), lambda i: (0, 0, (i + 1) * (MAIN // 128)))
+    rot, dil, tmp, pol, orders, limits = (
+        pltpu.with_memory_space_constraint(v, pltpu.HBM) for v in (rot, dil, tmp, pol, orders, limits)
+    )
     return pl.pallas_call(
         wind_legendre_kernel,
         grid=(STEPS,),
@@ -223,14 +212,14 @@
         out_specs=pl.BlockSpec((128, 16, 128), lambda i: (0, 0, 0)),
         out_shape=jax.ShapeDtypeStruct((128, 16, 128), BF16),
         scratch_shapes=[
-            pltpu.VMEM((8, MAIN + 128), BF16),
             pltpu.VMEM((16, MAIN + 128), BF16),
-            pltpu.VMEM((LATH, MAIN + 128), BF16),
+            pltpu.VMEM((LATH, WIN), BF16),
             pltpu.VMEM((GROUP, WIN), F32),
             pltpu.VMEM((GROUP, WIN), F32),
             pltpu.VMEM((GROUP, WIN), F32),
-            pltpu.VMEM((20 * KALL, LATH), F32),
-            pltpu.VMEM((20 * KALL, LATH), F32),
+            pltpu.VMEM((4, GROUP, WIN), F32),
+            pltpu.VMEM((12 * KALL, LATH), F32),
+            pltpu.VMEM((12 * KALL, LATH), F32),
             pltpu.VMEM((2048, 128), F32),
         ],
         compiler_params=pltpu.CompilerParams(vmem_limit_bytes=40 * 1024 * 1024),
@@ -377,6 +366,39 @@
     )(count, data, *tables)
 
 
+def unpack_kernel(rows, out_u, out_v, out_t, wide):
+    step = pl.program_id(0)
+
+    @pl.when(step == 0)
+    def _():
+        for slot in range(BAND_MAX):
+            for c in range(PIECE // 128):
+                lanes = slice(128 * c, 128 * c + 128)
+                wide[c, 96 * slot : 96 * slot + 96, :] = rows[slot, :, lanes].astype(F32)
+
+    for lv in range(2):
+        for fld, out in enumerate((out_u, out_v, out_t)):
+            for q in range(4):
+                row = lv * 48 + fld * 16 + q + step * 4
+                for c in range(PIECE // 128):
+                    lanes = slice(128 * c, 128 * c + 128)
+                    out[2 * q + lv, :, lanes] = wide[c, pl.ds(row, BAND_MAX, stride=96), :]
+
+
+def unpack(rows):
+    leaf = jax.ShapeDtypeStruct((LEVELS, BAND_MAX, PIECE), F32)
+    return pl.pallas_call(
+        unpack_kernel,
+        grid=(4,),
+        in_specs=[pl.BlockSpec((BAND_MAX, 96, PIECE), lambda i: (0, 0, 0))],
+        out_specs=[pl.BlockSpec((8, BAND_MAX, PIECE), lambda i: (i, 0, 0))] * 3,
+        out_shape=[leaf] * 3,
+        scratch_shapes=[pltpu.VMEM((PIECE // 128, BAND_MAX * 96, 128), F32)],
+        compiler_params=pltpu.CompilerParams(vmem_limit_bytes=24 * 1024 * 1024),
+        name="unpack",
+    )(rows)
+
+
 def wave_row(orders):
     lower = orders[:, 0::2]
     both = jnp.stack([lower, MW - 1 - lower], axis=1)
@@ -395,9 +417,7 @@
     tables = make_table(count, wave_row(orders))
     pieces = make_grid(count, got, tables)
     rows = lax.all_to_all(pieces, "ba", split_axis=0, concat_axis=0, tiled=True)
-    rows = rows.reshape(BAND_MAX, 2, 3, PIECES, PIECE).astype(F32)
-    outs = jnp.transpose(rows, (2, 3, 1, 0, 4)).reshape(3, LEVELS, BAND_MAX, PIECE)
-    return outs[0], outs[1], outs[2]
+    return tuple(unpack(rows))
 
 
 def solution(mesh):

time: 85.8 us -> 69.7 us (0.81)
  local copies, waits for them, and re-layouts: 13.9 us -> 1.03 us
  Pallas kernels: 28.3 us -> 25.3 us
    unnamed x18 -> x6, local copies, waits for them, and re-layouts: 8.58 us -> 0.01 us
    pallas_call x1, Pallas kernels: 20 us -> 14.3 us  [wind_legendre(): pl.pallas_call(wind_legendre_kernel, grid=(STEPS,), in_specs=[smem((8, 16...]
    slice x4 -> x0, local copies, waits for them, and re-layouts: 4.31 us -> none  [per_device(): return (outs[0], outs[1], outs[2])]
    pallas_call x0 -> x1, Pallas kernels: none -> 2.81 us  [unpack(): pl.pallas_call(unpack_kernel, grid=(4,), in_specs=[pl.BlockSpec((BAND_MAX...]
  transfers between devices with their start and end apart: 1 -> 1, of which waited for: 1 -> 1; matrix products, arithmetic and copies ran while one was open for 2% -> 2% of each run, Pallas kernels for 3% -> 4%
where the time goes in v2:
time: 69.7 us; the launch traced here: 69.2 us
  Pallas kernels  25.3 us (36%)
  blocking collectives  21.3 us (31%)
  starting transfers between devices  11.1 us (16%)
  waiting for transfers between devices  7.05 us (10%)
  between operations  2.68 us (4%)
  local copies, waits for them, and re-layouts  1.03 us (1%)
  other arithmetic  0.72 us (1%)
    all_to_all x1, blocking collectives, per_device(): rows = lax.all_to_all(pieces, 'ba', split_axis=0, concat_axis=0, tiled=True)  21.3 us
    pallas_call x1, Pallas kernels, wind_legendre(): pl.pallas_call(wind_legendre_kernel, grid=(STEPS,), in_specs=[smem((8, 16...  14.3 us
    all_to_all x1, starting transfers between devices, per_device(): lax.all_to_all(sent, ('aa', 'ba'), split_axis=0, concat_axis=0, tiled=True)  11.1 us
    all_to_all x1, waiting for transfers between devices, per_device(): lax.all_to_all(sent, ('aa', 'ba'), split_axis=0, concat_axis=0, tiled=True)  7.05 us
    pallas_call x1, Pallas kernels, make_grid(): pl.pallas_call(grid_kernel, grid=(PIECES // PSTEP,), in_specs=[pl.BlockSp...  5.45 us
    pallas_call x1, Pallas kernels, make_table(): pl.pallas_call(table_kernel, in_specs=[pl.BlockSpec(memory_space=pltpu.SM...  2.82 us
    pallas_call x1, Pallas kernels, unpack(): pl.pallas_call(unpack_kernel, grid=(4,), in_specs=[pl.BlockSpec((BAND_MAX...  2.81 us
  transfers between devices with their start and end apart: 1, of which 1 were waited for; matrix products, arithmetic and copies ran while one was open for 2% of the time, Pallas kernels for 4%

profile of v2, /device:TPU:0, one launch (start us, length us, event | category | flops | bytes accessed | tf_op | source)
XLA Modules:
  0.0 69.2 jit_solution(16698911433197554630)
XLA Ops:
  0.6 0.0 copy-start
  0.6 0.0 copy-start.1
  0.7 0.0 copy-start.2
  0.7 14.3 %wind_legendre.1 = bf16[128,16,128]{2,1,0:T(8,128)(2,1)} custom-call(s32[8,160]{1,0:T(8,128)} %orders.1, s32[9]{0:T(128)} %limits.1, s32[1]{0:T(128)} %bitcast.3.where_am_i, bf16[2,2,102480]{2,1,0:T(2,128)(2,1)} %rot_x.1, bf16[2,2,102480]{2,1,0:T(2,128)(2,1)} %rot_x.1, bf16[2,2,102480]{2,1,0:T(2,128)(2,1)} %dil_x.1, bf16[2,2,102480]{2,1,0:T(2,128)(2,1)} %dil_x.1, ...), custom_call_target="tpu_custom_call" | custom-call | tf_op jit(solution)/shard_map/wind_legendre/pallas_call | solution.py:196
  14.9 11.1 %all-to-all-start = ((bf16[128,16,128]{2,1,0:T(8,128)(2,1)}), bf16[128,16,128]{2,1,0:T(8,128)(2,1)S(1)}, u32[]{:S(2)}, u32[]{:S(2)}) async-start(bf16[128,16,128]{2,1,0:T(8,128)(2,1)} %wind_legendre.1), calls=%async_computation | async-start | bytes 1048576 | tf_op jit(solution)/shard_map/all_to_all | solution.py:412
  26.1 0.0 copy-done
  26.1 0.2 slice.17
  26.2 0.0 copy-done.1
  26.3 0.1 dynamic_slice.3
  26.4 0.1 reshape.12
  26.4 0.1 pad_add_fusion
  26.5 0.1 reshape.13
  26.6 0.6 fusion.1
  28.5 0.0 copy-done.2
  28.5 0.6 fusion
  29.8 2.8 %trig_table.1 = (bf16[2560,384]{1,0:T(8,128)(2,1)S(1)}, f32[16,1,1280]{2,1,0:T(1,128)S(1)}, f32[16,1,1280]{2,1,0:T(1,128)S(1)}, f32[8,1280]{1,0:T(8,128)S(1)}) custom-call(s32[1]{0:T(128)} %bitcast.2.count, s32[1,1280]{1,0:T(1,128)S(1)} %pad_add_fusion.1.wave), custom_call_target="tpu_custom_call" | custom-call | flops 50000000 | bytes 4000000 | tf_op jit(solution)/shard_map/trig_table/pallas_call | solution.py:272
  32.6 7.0 %all-to-all-done.data = bf16[128,16,128]{2,1,0:T(8,128)(2,1)S(1)} async-done(((bf16[128,16,128]{2,1,0:T(8,128)(2,1)}), bf16[128,16,128]{2,1,0:T(8,128)(2,1)S(1)}, u32[]{:S(2)}, u32[]{:S(2)}) %all-to-all-start) | async-done | bytes 524320 | tf_op jit(solution)/shard_map/all_to_all | solution.py:412
  39.7 5.4 %grid_product.1 = bf16[16,96,384]{2,1,0:T(8,128)(2,1)S(1)} custom-call(s32[1]{0:T(128)} %bitcast.2.count, bf16[128,16,128]{2,1,0:T(8,128)(2,1)S(1)} %all-to-all-done.data, bf16[2560,384]{1,0:T(8,128)(2,1)S(1)} %get-tuple-element.7.table, f32[16,1,1280]{2,1,0:T(1,128)S(1)} %get-tuple-element.8.twist_c, f32[16,1,1280]{2,1,0:T(1,128)S(1)} %get-tuple-element.9.twist_s, ...), custom_call_target="tpu_custom_call" | custom-call | tf_op jit(solution)/shard_map/grid_product/pallas_call | solution.py:346
  45.1 21.3 %all_to_all.10.rows = bf16[16,96,384]{2,1,0:T(8,128)(2,1)S(1)} all-to-all(bf16[16,96,384]{2,1,0:T(8,128)(2,1)S(1)} %grid_product.1), channel_id=1, replica_groups=mesh['aa'=8,'ba'=16] {'ba'}, dimensions={0} | all-to-all | bytes 2359296 | tf_op jit(solution)/shard_map/all_to_all | solution.py:419
  66.4 2.8 %unpack.1 = (f32[32,16,384]{2,1,0:T(8,128)}, f32[32,16,384]{2,1,0:T(8,128)}, f32[32,16,384]{2,1,0:T(8,128)}) custom-call(bf16[16,96,384]{2,1,0:T(8,128)(2,1)S(1)} %all_to_all.10.rows), custom_call_target="tpu_custom_call" | custom-call | tf_op jit(solution)/shard_map/unpack/pallas_call | solution.py:390
  (5 shorter events, 0.0 us)
Async XLA Ops:
  0.6 25.4 %copy-start = (s32[8,160]{1,0:T(8,128)S(1)}, s32[8,160]{1,0:T(8,128)}, u32[]{:S(2)}) copy-start(s32[8,160]{1,0:T(8,128)} %orders.1) | copy-start | bytes 15364
  0.6 25.6 %copy-start.1 = (s32[9]{0:T(128)S(1)}, s32[9]{0:T(128)}, u32[]{:S(2)}) copy-start(s32[9]{0:T(128)} %limits.1) | copy-start | bytes 112
  0.7 27.8 %copy-start.2 = (s32[96]{0:T(128)S(1)}, s32[96]{0:T(128)}, u32[]{:S(2)}) copy-start(s32[96]{0:T(128)} %param.12) | copy-start | bytes 1156
  14.9 24.8 %all-to-all-start = ((bf16[128,16,128]{2,1,0:T(8,128)(2,1)}), bf16[128,16,128]{2,1,0:T(8,128)(2,1)S(1)}, u32[]{:S(2)}, u32[]{:S(2)}) async-start(bf16[128,16,128]{2,1,0:T(8,128)(2,1)} %wind_legendre.1), calls=%async_computation | async-start | bytes 1048576 | tf_op jit(solution)/shard_map/all_to_all | solution.py:412

commit v3 on v2

--- a/solution.py
+++ b/solution.py
@@ -22,7 +22,8 @@
 LEVELS = 32
 KM = 64
 KR = PAIRS - KM
-KALL = 2 * PAIRS
+KALL = 2 * PAIRS + 1
+AHEAD = 2 * MAIN + 128
 F32 = jnp.float32
 BF16 = jnp.bfloat16
 NT = (((1,), (1,)), ((), ()))
@@ -33,16 +34,16 @@
     limits,
     where_am_i,
     rot,
+    dil,
+    tmp,
+    pol,
     rot_x,
-    dil,
     dil_x,
-    tmp,
     tmp_x,
-    pol,
     pol_x,
     out,
+    poly,
     fields,
-    last,
     coef_a,
     coef_b,
     coef_c,
@@ -50,23 +51,75 @@
     north,
     south,
     tiles,
+    sem_f,
+    sem_p,
 ):
-    step = pl.program_id(0)
     me = where_am_i[0]
-    live = 102480 - (step + 1) * MAIN
-
-    def edge(ref, lv):
-        lane2 = lax.broadcasted_iota(jnp.int32, (2, 128), 1)
-        return jnp.where(lane2 < live, ref[lv].astype(F32), 0.0).astype(BF16)
-
-    for src, (ref, ref_x) in enumerate(((rot, rot_x), (dil, dil_x), (tmp, tmp_x), (tmp, tmp_x))):
+    end = STEPS * MAIN
+
+    def field_copies(half):
+        lanes = pl.ds(0, AHEAD) if half == 0 else pl.ds(AHEAD, end - AHEAD)
+        for src, ref in enumerate((rot, dil, tmp, tmp)):
+            for lv in range(2):
+                rows = pl.ds(4 * src + 2 * lv, 2)
+                yield pltpu.make_async_copy(
+                    ref.at[lv, :, lanes], fields.at[rows, lanes], sem_f.at[half, 2 * src + lv]
+                )
+
+    def poly_copy(g, start, size):
+        lanes = pl.ds(start, size)
+        return pltpu.make_async_copy(pol.at[:, lanes], poly.at[:, lanes], sem_p.at[g])
+
+    def middle(g):
+        return poly_copy(g, pl.multiple_of(g * MAIN + 128, 128), MAIN)
+
+    first_poly = poly_copy(0, 0, MAIN + 128)
+    last_poly = poly_copy(STEPS - 1, (STEPS - 1) * MAIN + 128, MAIN - 128)
+    for copy in field_copies(0):
+        copy.start()
+    first_poly.start()
+    middle(1).start()
+    for copy in field_copies(1):
+        copy.start()
+    for g in range(2, STEPS - 1):
+        middle(g).start()
+    last_poly.start()
+
+    lane2 = lax.broadcasted_iota(jnp.int32, (2, 128), 1)
+    for src, ref in enumerate((rot_x, dil_x, tmp_x, tmp_x)):
         for lv in range(2):
-            row = src * 4 + lv * 2
-            fields[row : row + 2, 0:MAIN] = ref[lv]
-            fields[row : row + 2, MAIN : MAIN + 128] = edge(ref_x, lv)
-    last[:, 0:MW] = pol[:, MAIN - MW : MAIN]
+            edge = jnp.where(lane2 < PAIRS, ref[lv].astype(F32), 0.0).astype(BF16)
+            fields[4 * src + 2 * lv : 4 * src + 2 * lv + 2, end : end + 128] = edge
     lane48 = lax.broadcasted_iota(jnp.int32, (LATH, 128), 1)
-    last[:, MW:WIN] = jnp.where(lane48 < live, pol_x[...].astype(F32), 0.0).astype(BF16)
+    poly[:, end : end + 128] = jnp.where(lane48 < PAIRS, pol_x[...].astype(F32), 0.0).astype(BF16)
+
+    for copy in field_copies(0):
+        copy.wait()
+    first_poly.wait()
+
+    def group(step, carry):
+        @pl.when((step > 0) & (step < STEPS - 1))
+        def _():
+            middle(step).wait()
+
+        @pl.when(step == STEPS - 1)
+        def _():
+            last_poly.wait()
+
+        @pl.when(step == 2)
+        def _():
+            for copy in field_copies(1):
+                copy.wait()
+
+        one_group(step, me, orders, poly, fields, coef_a, coef_b, coef_c, masks, north, south)
+        return carry
+
+    lax.fori_loop(0, STEPS, group, 0)
+    pack_tiles(limits, out, north, south, tiles)
+
+
+def one_group(step, me, orders, poly, fields, coef_a, coef_b, coef_c, masks, north, south):
+    origin = pl.multiple_of(step * MAIN, 128)
 
     lane = lax.broadcasted_iota(jnp.int32, (GROUP, WIN), 1)
     sub = lax.broadcasted_iota(jnp.int32, (GROUP, WIN), 0)
@@ -81,11 +134,8 @@
     first = pos < MW - lower
     wave_i = jnp.where(first, lower, MW - 1 - lower)
     deg_i = jnp.where(first, lower + pos, pos - 1)
-    even = ((deg_i - wave_i) & 1) == 0
-    masks[0] = jnp.where(valid & first & even, 1.0, 0.0)
-    masks[1] = jnp.where(valid & first & ~even, 1.0, 0.0)
-    masks[2] = jnp.where(valid & ~first & even, 1.0, 0.0)
-    masks[3] = jnp.where(valid & ~first & ~even, 1.0, 0.0)
+    masks[0] = jnp.where(valid & first, 1.0, 0.0)
+    masks[1] = jnp.where(valid & ~first, 1.0, 0.0)
     wave = wave_i.astype(F32)
     usable = valid & (deg_i > 0)
     deg = jnp.where(usable, deg_i, 1).astype(F32)
@@ -102,17 +152,25 @@
     base = jnp.where(early, step * GROUP, 2 * KM + (step - KM // GROUP) * GROUP)
     seg_off = jnp.where(early, KM, KR)
 
-    row8 = lax.broadcasted_iota(jnp.int32, (8, WIN), 0)
-    row_even = (row8 & 1) == 0
-    top_half = row8 < 4
-    sign = jnp.where(row_even == top_half, 1.0, -1.0)
+    def wide(tile):
+        return jnp.concatenate([tile] * (WIN // 128), axis=1)
+
+    row8 = lax.broadcasted_iota(jnp.int32, (8, 128), 0)
+    row_even = wide((row8 & 1) == 0)
+    sign = wide(jnp.where(((row8 & 1) == 0) == (row8 < 4), 1.0, -1.0))
+    row16 = lax.broadcasted_iota(jnp.int32, (16, 128), 0)
+    lane16 = lax.broadcasted_iota(jnp.int32, (16, 128), 1)
+    alternate = jnp.where((lane16 & 1) == 0, 1.0, -1.0)
+    flip_wind = wide(alternate.astype(BF16))
+    flip_heat = wide(jnp.where(row16 % 8 < 4, 1.0, alternate).astype(BF16))
 
     def spread(ref, s):
         return ref[pl.ds(s, 8, stride=0), :]
 
+    results = []
     for s in range(GROUP):
-        lo = s * MW
-        both = fields[:, lo : lo + WIN].astype(F32)
+        window = pl.ds(pl.multiple_of(origin + s * MW, 128), WIN)
+        both = fields[:, window].astype(F32)
         x, heat = both[0:8], both[8:16]
         other = jnp.where(row_even, pltpu.roll(x, 3, 0), pltpu.roll(x, 5, 0))
         wind = (
@@ -120,111 +178,110 @@
             - spread(coef_a, s) * pltpu.roll(x, 1, 1)
             + spread(coef_c, s) * (other * sign)
         )
-        m = [spread(masks.at[g], s) for g in range(4)]
-        rows = [wind * m[g] for g in range(4)]
-        rows.append(heat * jnp.where(top_half, m[0], m[1]))
-        rows.append(heat * jnp.where(top_half, m[2], m[3]))
-        data = jnp.concatenate(rows, axis=0).astype(BF16)
-        poly = last[...] if s == GROUP - 1 else pol[:, lo : lo + WIN]
-        res = lax.dot_general(data, poly, NT, preferred_element_type=F32)
+        m0, m1 = spread(masks.at[0], s), spread(masks.at[1], s)
+        winds = jnp.concatenate([wind * m0, wind * m1], axis=0).astype(BF16)
+        heats = jnp.concatenate([heat * m0, heat * m1], axis=0).astype(BF16)
+        data = jnp.concatenate([winds, winds * flip_wind, heats * flip_heat], axis=0)
+        results.append(lax.dot_general(data, poly[:, window], NT, preferred_element_type=F32))
+    for s, res in enumerate(results):
+        pair = step * GROUP + s
+        odd = (pair & 1, (pair + low[s]) & 1)
         for seg in range(2):
             at = base + s + seg * seg_off
-            plus = res[seg * 16 : seg * 16 + 8]
-            minus = res[seg * 16 + 8 : seg * 16 + 16]
-            north[pl.ds(at, 8, stride=KALL), :] = plus + minus
-            south[pl.ds(at, 8, stride=KALL), :] = plus - minus
-            pair = res[32 + seg * 8 : 40 + seg * 8]
-            flip = pltpu.roll(pair, 4, 0)
-            north[pl.ds(8 * KALL + at, 4, stride=KALL), :] = (pair + flip)[0:4]
-            south[pl.ds(8 * KALL + at, 4, stride=KALL), :] = (pair - flip)[0:4]
-
-    @pl.when(step == STEPS - 1)
-    def _():
-        dest = lax.broadcasted_iota(jnp.int32, (128, LATH), 0)
-        column = lax.broadcasted_iota(jnp.int32, (128, LATH), 1)
-        lat = dest % BAND_MAX
-        for band in range(8):
-            lat = lat + jnp.where(dest // BAND_MAX == band, limits[band], 0)
-        pick_n = (lat == column).astype(F32).astype(BF16)
-        pick_s = (2 * LATH - 1 - lat == column).astype(F32).astype(BF16)
-
-        def rows_of(ref, part, lv, fld, start, size):
-            row = fld * 4 + lv * 2 + part
-            val = ref[row * KALL + start : row * KALL + start + size, :]
-            return (-val if fld == 1 else val).astype(BF16)
-
-        def select(rows_n, rows_s, row):
-            val = lax.dot_general(pick_n, rows_n, NT, preferred_element_type=F32)
-            val = val + lax.dot_general(pick_s, rows_s, NT, preferred_element_type=F32)
-            for block in range(16):
-                tiles[pl.ds(row + 128 * block, 8, stride=16), :] = val[8 * block : 8 * block + 8]
-
-        for part in range(2):
-            for lv in range(2):
-                for fld in range(3):
-                    select(
-                        rows_of(north, part, lv, fld, 0, 2 * KM),
-                        rows_of(south, part, lv, fld, 0, 2 * KM),
-                        part * 6 + lv * 3 + fld,
-                    )
-        for fld in range(3):
-            both = []
-            for ref in (north, south):
-                both.append(
-                    jnp.concatenate(
-                        [rows_of(ref, q // 2, q % 2, fld, 2 * KM, 2 * KR) for q in range(4)],
-                        axis=0,
-                    )
+            factor = (1 - 2 * odd[seg]).astype(F32)
+            north[pl.ds(at, 8, stride=KALL), :] = res[seg * 8 : seg * 8 + 8]
+            south[pl.ds(at, 8, stride=KALL), :] = res[16 + seg * 8 : 24 + seg * 8] * factor
+            heat = res[32 + seg * 8 : 40 + seg * 8]
+            north[pl.ds(8 * KALL + at, 4, stride=KALL), :] = heat[0:4]
+            south[pl.ds(8 * KALL + at, 4, stride=KALL), :] = heat[4:8] * factor
+
+
+def pack_tiles(limits, out, north, south, tiles):
+    dest = lax.broadcasted_iota(jnp.int32, (128, LATH), 0)
+    column = lax.broadcasted_iota(jnp.int32, (128, LATH), 1)
+    lat = dest % BAND_MAX
+    for band in range(8):
+        lat = lat + jnp.where(dest // BAND_MAX == band, limits[band], 0)
+    pick_n = (lat == column).astype(F32).astype(BF16)
+    pick_s = (2 * LATH - 1 - lat == column).astype(F32).astype(BF16)
+
+    def rows_of(ref, part, lv, fld, start, size):
+        row = fld * 4 + lv * 2 + part
+        val = ref[row * KALL + start : row * KALL + start + size, :]
+        return (-val if fld == 1 else val).astype(BF16)
+
+    def select(rows_n, rows_s, row):
+        val = lax.dot_general(pick_n, rows_n, NT, preferred_element_type=F32)
+        val = val + lax.dot_general(pick_s, rows_s, NT, preferred_element_type=F32)
+        for block in range(16):
+            tiles[pl.ds(row + 128 * block, 8, stride=16), :] = val[8 * block : 8 * block + 8]
+
+    for part in range(2):
+        for lv in range(2):
+            for fld in range(3):
+                select(
+                    rows_of(north, part, lv, fld, 0, 2 * KM),
+                    rows_of(south, part, lv, fld, 0, 2 * KM),
+                    part * 6 + lv * 3 + fld,
                 )
-            select(both[0], both[1], 12 + fld)
-        for block in range(16):
-            tiles[pl.ds(15 + 128 * block, 8, stride=16), :] = jnp.zeros((8, 128), F32)
-        for block in range(16):
-            part = tiles[128 * block : 128 * block + 128, :]
-            out[8 * block : 8 * block + 8] = part.reshape(8, 16, 128).astype(BF16)
+    for fld in range(3):
+        both = []
+        for ref in (north, south):
+            both.append(
+                jnp.concatenate(
+                    [rows_of(ref, q // 2, q % 2, fld, 2 * KM, 2 * KR) for q in range(4)],
+                    axis=0,
+                )
+            )
+        select(both[0], both[1], 12 + fld)
+    for block in range(16):
+        tiles[pl.ds(15 + 128 * block, 8, stride=16), :] = jnp.zeros((8, 128), F32)
+    for block in range(16):
+        part = tiles[128 * block : 128 * block + 128, :]
+        out[8 * block : 8 * block + 8] = part.reshape(8, 16, 128).astype(BF16)
 
 
 def wind_legendre(rot, dil, tmp, pol, orders, limits, me):
-    def smem(shape):
-        return pl.BlockSpec(shape, lambda i: (0,) * len(shape), memory_space=pltpu.SMEM)
-
-    main = pl.BlockSpec((2, 2, MAIN), lambda i: (0, 0, i))
-    tail = pl.BlockSpec((2, 2, 128), lambda i: (0, 0, (i + 1) * (MAIN // 128)))
     rot, dil, tmp, pol, orders, limits = (
         pltpu.with_memory_space_constraint(v, pltpu.HBM) for v in (rot, dil, tmp, pol, orders, limits)
     )
+    smem = pl.BlockSpec(memory_space=pltpu.SMEM)
+    hbm = pl.BlockSpec(memory_space=pltpu.HBM)
+    tail = pl.BlockSpec((2, 2, 128), lambda i: (0, 0, PAIRS * MW // 128))
     return pl.pallas_call(
         wind_legendre_kernel,
-        grid=(STEPS,),
+        grid=(1,),
         in_specs=[
-            smem((8, 160)),
-            smem((9,)),
-            smem((1,)),
-            main,
+            smem,
+            smem,
+            smem,
+            hbm,
+            hbm,
+            hbm,
+            hbm,
             tail,
-            main,
             tail,
-            main,
             tail,
-            pl.BlockSpec((LATH, MAIN), lambda i: (0, i)),
-            pl.BlockSpec((LATH, 128), lambda i: (0, (i + 1) * (MAIN // 128))),
+            pl.BlockSpec((LATH, 128), lambda i: (0, PAIRS * MW // 128)),
         ],
         out_specs=pl.BlockSpec((128, 16, 128), lambda i: (0, 0, 0)),
         out_shape=jax.ShapeDtypeStruct((128, 16, 128), BF16),
         scratch_shapes=[
-            pltpu.VMEM((16, MAIN + 128), BF16),
-            pltpu.VMEM((LATH, WIN), BF16),
+            pltpu.VMEM((LATH, STEPS * MAIN + 128), BF16),
+            pltpu.VMEM((16, STEPS * MAIN + 128), BF16),
             pltpu.VMEM((GROUP, WIN), F32),
             pltpu.VMEM((GROUP, WIN), F32),
             pltpu.VMEM((GROUP, WIN), F32),
-            pltpu.VMEM((4, GROUP, WIN), F32),
+            pltpu.VMEM((2, GROUP, WIN), F32),
             pltpu.VMEM((12 * KALL, LATH), F32),
             pltpu.VMEM((12 * KALL, LATH), F32),
             pltpu.VMEM((2048, 128), F32),
+            pltpu.SemaphoreType.DMA((2, 8)),
+            pltpu.SemaphoreType.DMA((STEPS,)),
         ],
         compiler_params=pltpu.CompilerParams(vmem_limit_bytes=40 * 1024 * 1024),
         name="wind_legendre",
-    )(orders, limits, me, rot, rot, dil, dil, tmp, tmp, pol, pol)
+    )(orders, limits, me, rot, dil, tmp, pol, rot, dil, tmp, pol)
 
 
 def cos_sin_turns(turns):
@@ -367,33 +424,24 @@
 
 
 def unpack_kernel(rows, out_u, out_v, out_t, wide):
-    step = pl.program_id(0)
-
-    @pl.when(step == 0)
-    def _():
-        for slot in range(BAND_MAX):
-            for c in range(PIECE // 128):
-                lanes = slice(128 * c, 128 * c + 128)
-                wide[c, 96 * slot : 96 * slot + 96, :] = rows[slot, :, lanes].astype(F32)
-
+    for slot in range(BAND_MAX):
+        wide[97 * slot : 97 * slot + 96, :] = rows[slot].astype(F32)
     for lv in range(2):
         for fld, out in enumerate((out_u, out_v, out_t)):
-            for q in range(4):
-                row = lv * 48 + fld * 16 + q + step * 4
-                for c in range(PIECE // 128):
-                    lanes = slice(128 * c, 128 * c + 128)
-                    out[2 * q + lv, :, lanes] = wide[c, pl.ds(row, BAND_MAX, stride=96), :]
+            for src in range(16):
+                row = lv * 48 + fld * 16 + src
+                out[2 * src + lv] = wide[pl.ds(row, BAND_MAX, stride=97), :]
 
 
 def unpack(rows):
     leaf = jax.ShapeDtypeStruct((LEVELS, BAND_MAX, PIECE), F32)
     return pl.pallas_call(
         unpack_kernel,
-        grid=(4,),
-        in_specs=[pl.BlockSpec((BAND_MAX, 96, PIECE), lambda i: (0, 0, 0))],
-        out_specs=[pl.BlockSpec((8, BAND_MAX, PIECE), lambda i: (i, 0, 0))] * 3,
+        grid=(PIECE // 128,),
+        in_specs=[pl.BlockSpec((BAND_MAX, 96, 128), lambda i: (0, 0, i))],
+        out_specs=[pl.BlockSpec((LEVELS, BAND_MAX, 128), lambda i: (0, 0, i))] * 3,
         out_shape=[leaf] * 3,
-        scratch_shapes=[pltpu.VMEM((PIECE // 128, BAND_MAX * 96, 128), F32)],
+        scratch_shapes=[pltpu.VMEM((BAND_MAX * 97, 128), F32)],
         compiler_params=pltpu.CompilerParams(vmem_limit_bytes=24 * 1024 * 1024),
         name="unpack",
     )(rows)

time: 69.7 us -> 67.4 us (0.967)
  Pallas kernels: 25.3 us -> 23.2 us
    pallas_call x2, Pallas kernels: 17.1 us -> 14.9 us  [the longest x1 12.9 us: wind_legendre(): pl.pallas_call(wind_legendre_kernel, grid=(1,), in_specs=[smem, smem, sme...]
  transfers between devices with their start and end apart: 1 -> 1, of which waited for: 1 -> 1; matrix products, arithmetic and copies ran while one was open for 2% -> 3% of each run, Pallas kernels for 4% -> 4%
where the time goes in v3:
time: 67.4 us; the launch traced here: 67.1 us
  Pallas kernels  23.2 us (34%)
  blocking collectives  21.3 us (32%)
  starting transfers between devices  11.2 us (17%)
  waiting for transfers between devices  7.05 us (10%)
  between operations  2.69 us (4%)
  local copies, waits for them, and re-layouts  1.03 us (2%)
  other arithmetic  0.72 us (1%)
    all_to_all x1, blocking collectives, per_device(): rows = lax.all_to_all(pieces, 'ba', split_axis=0, concat_axis=0, tiled=True)  21.3 us
    pallas_call x1, Pallas kernels, wind_legendre(): pl.pallas_call(wind_legendre_kernel, grid=(1,), in_specs=[smem, smem, sme...  12.9 us
    all_to_all x1, starting transfers between devices, per_device(): lax.all_to_all(sent, ('aa', 'ba'), split_axis=0, concat_axis=0, tiled=True)  11.2 us
    all_to_all x1, waiting for transfers between devices, per_device(): lax.all_to_all(sent, ('aa', 'ba'), split_axis=0, concat_axis=0, tiled=True)  7.05 us
    pallas_call x1, Pallas kernels, make_grid(): pl.pallas_call(grid_kernel, grid=(PIECES // PSTEP,), in_specs=[pl.BlockSp...  5.45 us
    pallas_call x1, Pallas kernels, make_table(): pl.pallas_call(table_kernel, in_specs=[pl.BlockSpec(memory_space=pltpu.SM...  2.82 us
    pallas_call x1, Pallas kernels, unpack(): pl.pallas_call(unpack_kernel, grid=(PIECE // 128,), in_specs=[pl.BlockSpe...  2.02 us
  transfers between devices with their start and end apart: 1, of which 1 were waited for; matrix products, arithmetic and copies ran while one was open for 3% of the time, Pallas kernels for 4%

profile of v3, /device:TPU:0, one launch (start us, length us, event | category | flops | bytes accessed | tf_op | source)
XLA Modules:
  0.0 67.1 jit_solution(6160905931652911053)
XLA Ops:
  0.6 0.0 copy-start
  0.6 0.0 copy-start.1
  0.7 0.0 copy-start.2
  0.7 12.9 %wind_legendre.1 = bf16[128,16,128]{2,1,0:T(8,128)(2,1)} custom-call(s32[8,160]{1,0:T(8,128)} %orders.1, s32[9]{0:T(128)} %limits.1, s32[1]{0:T(128)} %bitcast.3.where_am_i, bf16[2,2,102480]{2,1,0:T(2,128)(2,1)} %rot_x.1, bf16[2,2,102480]{2,1,0:T(2,128)(2,1)} %dil_x.1, bf16[2,2,102480]{2,1,0:T(2,128)(2,1)} %tmp_x.1, bf16[48,102480]{1,0:T(8,128)(2,1)} %pol_x.1, ...), custom_call_target="tpu_custom_call" | custom-call | tf_op jit(solution)/shard_map/wind_legendre/pallas_call | solution.py:251
  13.6 11.2 %all-to-all-start = ((bf16[128,16,128]{2,1,0:T(8,128)(2,1)}), bf16[128,16,128]{2,1,0:T(8,128)(2,1)S(1)}, u32[]{:S(2)}, u32[]{:S(2)}) async-start(bf16[128,16,128]{2,1,0:T(8,128)(2,1)} %wind_legendre.1), calls=%async_computation | async-start | bytes 1048576 | tf_op jit(solution)/shard_map/all_to_all | solution.py:460
  24.8 0.0 copy-done
  24.8 0.2 slice.17
  24.9 0.0 copy-done.1
  24.9 0.1 dynamic_slice.3
  25.0 0.1 reshape.12
  25.1 0.1 pad_add_fusion
  25.2 0.1 reshape.13
  25.3 0.6 fusion.1
  27.2 0.0 copy-done.2
  27.2 0.6 fusion
  28.5 2.8 %trig_table.1 = (bf16[2560,384]{1,0:T(8,128)(2,1)S(1)}, f32[16,1,1280]{2,1,0:T(1,128)S(1)}, f32[16,1,1280]{2,1,0:T(1,128)S(1)}, f32[8,1280]{1,0:T(8,128)S(1)}) custom-call(s32[1]{0:T(128)} %bitcast.2.count, s32[1,1280]{1,0:T(1,128)S(1)} %pad_add_fusion.1.wave), custom_call_target="tpu_custom_call" | custom-call | flops 50000000 | bytes 4000000 | tf_op jit(solution)/shard_map/trig_table/pallas_call | solution.py:329
  31.3 7.0 %all-to-all-done.data = bf16[128,16,128]{2,1,0:T(8,128)(2,1)S(1)} async-done(((bf16[128,16,128]{2,1,0:T(8,128)(2,1)}), bf16[128,16,128]{2,1,0:T(8,128)(2,1)S(1)}, u32[]{:S(2)}, u32[]{:S(2)}) %all-to-all-start) | async-done | bytes 524320 | tf_op jit(solution)/shard_map/all_to_all | solution.py:460
  38.4 5.4 %grid_product.1 = bf16[16,96,384]{2,1,0:T(8,128)(2,1)S(1)} custom-call(s32[1]{0:T(128)} %bitcast.2.count, bf16[128,16,128]{2,1,0:T(8,128)(2,1)S(1)} %all-to-all-done.data, bf16[2560,384]{1,0:T(8,128)(2,1)S(1)} %get-tuple-element.7.table, f32[16,1,1280]{2,1,0:T(1,128)S(1)} %get-tuple-element.8.twist_c, f32[16,1,1280]{2,1,0:T(1,128)S(1)} %get-tuple-element.9.twist_s, ...), custom_call_target="tpu_custom_call" | custom-call | tf_op jit(solution)/shard_map/grid_product/pallas_call | solution.py:403
  43.8 21.3 %all_to_all.10.rows = bf16[16,96,384]{2,1,0:T(8,128)(2,1)S(1)} all-to-all(bf16[16,96,384]{2,1,0:T(8,128)(2,1)S(1)} %grid_product.1), channel_id=1, replica_groups=mesh['aa'=8,'ba'=16] {'ba'}, dimensions={0} | all-to-all | bytes 2359296 | tf_op jit(solution)/shard_map/all_to_all | solution.py:467
  65.1 2.0 %unpack.1 = (f32[32,16,384]{2,1,0:T(8,128)}, f32[32,16,384]{2,1,0:T(8,128)}, f32[32,16,384]{2,1,0:T(8,128)}) custom-call(bf16[16,96,384]{2,1,0:T(8,128)(2,1)S(1)} %all_to_all.10.rows), custom_call_target="tpu_custom_call" | custom-call | tf_op jit(solution)/shard_map/unpack/pallas_call | solution.py:438
  (5 shorter events, 0.0 us)
Async XLA Ops:
  0.6 24.1 %copy-start = (s32[8,160]{1,0:T(8,128)S(1)}, s32[8,160]{1,0:T(8,128)}, u32[]{:S(2)}) copy-start(s32[8,160]{1,0:T(8,128)} %orders.1) | copy-start | bytes 15364
  0.6 24.3 %copy-start.1 = (s32[9]{0:T(128)S(1)}, s32[9]{0:T(128)}, u32[]{:S(2)}) copy-start(s32[9]{0:T(128)} %limits.1) | copy-start | bytes 112
  0.7 26.5 %copy-start.2 = (s32[96]{0:T(128)S(1)}, s32[96]{0:T(128)}, u32[]{:S(2)}) copy-start(s32[96]{0:T(128)} %param.12) | copy-start | bytes 1156
  13.6 24.8 %all-to-all-start = ((bf16[128,16,128]{2,1,0:T(8,128)(2,1)}), bf16[128,16,128]{2,1,0:T(8,128)(2,1)S(1)}, u32[]{:S(2)}, u32[]{:S(2)}) async-start(bf16[128,16,128]{2,1,0:T(8,128)(2,1)} %wind_legendre.1), calls=%async_computation | async-start | bytes 1048576 | tf_op jit(solution)/shard_map/all_to_all | solution.py:460

commit v4 on v3

--- a/solution.py
+++ b/solution.py
@@ -11,7 +11,7 @@
 MW = 1280
 WIDTH = MW + 1
 PAIRS = 80
-GROUP = 8
+GROUP = 16
 STEPS = PAIRS // GROUP
 MAIN = GROUP * MW
 WIN = 1408
@@ -23,7 +23,10 @@
 KM = 64
 KR = PAIRS - KM
 KALL = 2 * PAIRS + 1
-AHEAD = 2 * MAIN + 128
+BLOCK = 16
+BLOCKS = PAIRS // BLOCK
+PART = BLOCK * MW
+AHEAD = 2
 F32 = jnp.float32
 BF16 = jnp.bfloat16
 NT = (((1,), (1,)), ((), ()))
@@ -57,33 +60,30 @@
     me = where_am_i[0]
     end = STEPS * MAIN
 
-    def field_copies(half):
-        lanes = pl.ds(0, AHEAD) if half == 0 else pl.ds(AHEAD, end - AHEAD)
+    def span(g, start, size):
+        lanes = pl.ds(start, size)
         for src, ref in enumerate((rot, dil, tmp, tmp)):
             for lv in range(2):
                 rows = pl.ds(4 * src + 2 * lv, 2)
                 yield pltpu.make_async_copy(
-                    ref.at[lv, :, lanes], fields.at[rows, lanes], sem_f.at[half, 2 * src + lv]
+                    ref.at[lv, :, lanes], fields.at[rows, lanes], sem_f.at[2 * src + lv, g]
                 )
-
-    def poly_copy(g, start, size):
-        lanes = pl.ds(start, size)
-        return pltpu.make_async_copy(pol.at[:, lanes], poly.at[:, lanes], sem_p.at[g])
-
-    def middle(g):
-        return poly_copy(g, pl.multiple_of(g * MAIN + 128, 128), MAIN)
-
-    first_poly = poly_copy(0, 0, MAIN + 128)
-    last_poly = poly_copy(STEPS - 1, (STEPS - 1) * MAIN + 128, MAIN - 128)
-    for copy in field_copies(0):
+        yield pltpu.make_async_copy(pol.at[:, lanes], poly.at[:, lanes], sem_p.at[g])
+
+    def copies(g):
+        return span(g, pl.multiple_of(g * PART + 128, 128), PART)
+
+    def first_copies():
+        return span(0, 0, PART + 128)
+
+    def last_copies():
+        return span(BLOCKS - 1, (BLOCKS - 1) * PART + 128, PART - 128)
+
+    for copy in first_copies():
         copy.start()
-    first_poly.start()
-    middle(1).start()
-    for copy in field_copies(1):
-        copy.start()
-    for g in range(2, STEPS - 1):
-        middle(g).start()
-    last_poly.start()
+    for g in range(1, AHEAD):
+        for copy in copies(g):
+            copy.start()
 
     lane2 = lax.broadcasted_iota(jnp.int32, (2, 128), 1)
     for src, ref in enumerate((rot_x, dil_x, tmp_x, tmp_x)):
@@ -93,32 +93,39 @@
     lane48 = lax.broadcasted_iota(jnp.int32, (LATH, 128), 1)
     poly[:, end : end + 128] = jnp.where(lane48 < PAIRS, pol_x[...].astype(F32), 0.0).astype(BF16)
 
-    for copy in field_copies(0):
+    for copy in first_copies():
         copy.wait()
-    first_poly.wait()
+
+    def turn(block):
+        @pl.when((block > 0) & (block < BLOCKS - 1))
+        def _():
+            for copy in copies(block):
+                copy.wait()
+
+        @pl.when(block == BLOCKS - 1)
+        def _():
+            for copy in last_copies():
+                copy.wait()
+
+        @pl.when(block + AHEAD < BLOCKS - 1)
+        def _():
+            for copy in copies(block + AHEAD):
+                copy.start()
+
+        @pl.when(block + AHEAD == BLOCKS - 1)
+        def _():
+            for copy in last_copies():
+                copy.start()
 
     def group(step, carry):
-        @pl.when((step > 0) & (step < STEPS - 1))
-        def _():
-            middle(step).wait()
-
-        @pl.when(step == STEPS - 1)
-        def _():
-            last_poly.wait()
-
-        @pl.when(step == 2)
-        def _():
-            for copy in field_copies(1):
-                copy.wait()
-
-        one_group(step, me, orders, poly, fields, coef_a, coef_b, coef_c, masks, north, south)
+        one_group(step, turn, me, orders, poly, fields, coef_a, coef_b, coef_c, masks, north, south)
         return carry
 
     lax.fori_loop(0, STEPS, group, 0)
     pack_tiles(limits, out, north, south, tiles)
 
 
-def one_group(step, me, orders, poly, fields, coef_a, coef_b, coef_c, masks, north, south):
+def one_group(step, turn, me, orders, poly, fields, coef_a, coef_b, coef_c, masks, north, south):
     origin = pl.multiple_of(step * MAIN, 128)
 
     lane = lax.broadcasted_iota(jnp.int32, (GROUP, WIN), 1)
@@ -169,6 +176,8 @@
 
     results = []
     for s in range(GROUP):
+        if s % BLOCK == 0:
+            turn(step * (GROUP // BLOCK) + s // BLOCK)
         window = pl.ds(pl.multiple_of(origin + s * MW, 128), WIN)
         both = fields[:, window].astype(F32)
         x, heat = both[0:8], both[8:16]
@@ -276,8 +285,8 @@
             pltpu.VMEM((12 * KALL, LATH), F32),
             pltpu.VMEM((12 * KALL, LATH), F32),
             pltpu.VMEM((2048, 128), F32),
-            pltpu.SemaphoreType.DMA((2, 8)),
-            pltpu.SemaphoreType.DMA((STEPS,)),
+            pltpu.SemaphoreType.DMA((8, BLOCKS)),
+            pltpu.SemaphoreType.DMA((BLOCKS,)),
         ],
         compiler_params=pltpu.CompilerParams(vmem_limit_bytes=40 * 1024 * 1024),
         name="wind_legendre",

time: 67.4 us -> 65.7 us (0.975)
  Pallas kernels: 23.2 us -> 21.6 us
    pallas_call x1, Pallas kernels: 12.9 us -> 11.3 us  [wind_legendre(): pl.pallas_call(wind_legendre_kernel, grid=(1,), in_specs=[smem, smem, sme...]
where the time goes in v4:
time: 65.7 us; the launch traced here: 65.4 us
  Pallas kernels  21.6 us (33%)
  blocking collectives  21.3 us (32%)
  starting transfers between devices  11.1 us (17%)
  waiting for transfers between devices  7.05 us (11%)
  between operations  2.69 us (4%)
  local copies, waits for them, and re-layouts  1.03 us (2%)
  other arithmetic  0.72 us (1%)
    all_to_all x1, blocking collectives, per_device(): rows = lax.all_to_all(pieces, 'ba', split_axis=0, concat_axis=0, tiled=True)  21.3 us
    pallas_call x1, Pallas kernels, wind_legendre(): pl.pallas_call(wind_legendre_kernel, grid=(1,), in_specs=[smem, smem, sme...  11.3 us
    all_to_all x1, starting transfers between devices, per_device(): lax.all_to_all(sent, ('aa', 'ba'), split_axis=0, concat_axis=0, tiled=True)  11.1 us
    all_to_all x1, waiting for transfers between devices, per_device(): lax.all_to_all(sent, ('aa', 'ba'), split_axis=0, concat_axis=0, tiled=True)  7.05 us
    pallas_call x1, Pallas kernels, make_grid(): pl.pallas_call(grid_kernel, grid=(PIECES // PSTEP,), in_specs=[pl.BlockSp...  5.45 us
    pallas_call x1, Pallas kernels, make_table(): pl.pallas_call(table_kernel, in_specs=[pl.BlockSpec(memory_space=pltpu.SM...  2.82 us
    pallas_call x1, Pallas kernels, unpack(): pl.pallas_call(unpack_kernel, grid=(PIECE // 128,), in_specs=[pl.BlockSpe...  2.02 us
  transfers between devices with their start and end apart: 1, of which 1 were waited for; matrix products, arithmetic and copies ran while one was open for 3% of the time, Pallas kernels for 4%

profile of v4, /device:TPU:0, one launch (start us, length us, event | category | flops | bytes accessed | tf_op | source)
XLA Modules:
  0.0 65.4 jit_solution(12745644915217625003)
XLA Ops:
  0.6 0.0 copy-start
  0.6 0.0 copy-start.1
  0.7 0.0 copy-start.2
  0.7 11.3 %wind_legendre.1 = bf16[128,16,128]{2,1,0:T(8,128)(2,1)} custom-call(s32[8,160]{1,0:T(8,128)} %orders.1, s32[9]{0:T(128)} %limits.1, s32[1]{0:T(128)} %bitcast.3.where_am_i, bf16[2,2,102480]{2,1,0:T(2,128)(2,1)} %rot_x.1, bf16[2,2,102480]{2,1,0:T(2,128)(2,1)} %dil_x.1, bf16[2,2,102480]{2,1,0:T(2,128)(2,1)} %tmp_x.1, bf16[48,102480]{1,0:T(8,128)(2,1)} %pol_x.1, ...), custom_call_target="tpu_custom_call" | custom-call | tf_op jit(solution)/shard_map/wind_legendre/pallas_call | solution.py:260
  11.9 11.1 %all-to-all-start = ((bf16[128,16,128]{2,1,0:T(8,128)(2,1)}), bf16[128,16,128]{2,1,0:T(8,128)(2,1)S(1)}, u32[]{:S(2)}, u32[]{:S(2)}) async-start(bf16[128,16,128]{2,1,0:T(8,128)(2,1)} %wind_legendre.1), calls=%async_computation | async-start | bytes 1048576 | tf_op jit(solution)/shard_map/all_to_all | solution.py:469
  23.1 0.0 copy-done
  23.1 0.2 slice.17
  23.3 0.0 copy-done.1
  23.3 0.1 dynamic_slice.3
  23.4 0.1 reshape.12
  23.5 0.1 pad_add_fusion
  23.5 0.1 reshape.13
  23.6 0.6 fusion.1
  25.5 0.0 copy-done.2
  25.5 0.6 fusion
  26.8 2.8 %trig_table.1 = (bf16[2560,384]{1,0:T(8,128)(2,1)S(1)}, f32[16,1,1280]{2,1,0:T(1,128)S(1)}, f32[16,1,1280]{2,1,0:T(1,128)S(1)}, f32[8,1280]{1,0:T(8,128)S(1)}) custom-call(s32[1]{0:T(128)} %bitcast.2.count, s32[1,1280]{1,0:T(1,128)S(1)} %pad_add_fusion.1.wave), custom_call_target="tpu_custom_call" | custom-call | flops 50000000 | bytes 4000000 | tf_op jit(solution)/shard_map/trig_table/pallas_call | solution.py:338
  29.7 7.0 %all-to-all-done.data = bf16[128,16,128]{2,1,0:T(8,128)(2,1)S(1)} async-done(((bf16[128,16,128]{2,1,0:T(8,128)(2,1)}), bf16[128,16,128]{2,1,0:T(8,128)(2,1)S(1)}, u32[]{:S(2)}, u32[]{:S(2)}) %all-to-all-start) | async-done | bytes 524320 | tf_op jit(solution)/shard_map/all_to_all | solution.py:469
  36.7 5.4 %grid_product.1 = bf16[16,96,384]{2,1,0:T(8,128)(2,1)S(1)} custom-call(s32[1]{0:T(128)} %bitcast.2.count, bf16[128,16,128]{2,1,0:T(8,128)(2,1)S(1)} %all-to-all-done.data, bf16[2560,384]{1,0:T(8,128)(2,1)S(1)} %get-tuple-element.7.table, f32[16,1,1280]{2,1,0:T(1,128)S(1)} %get-tuple-element.8.twist_c, f32[16,1,1280]{2,1,0:T(1,128)S(1)} %get-tuple-element.9.twist_s, ...), custom_call_target="tpu_custom_call" | custom-call | tf_op jit(solution)/shard_map/grid_product/pallas_call | solution.py:412
  42.2 21.3 %all_to_all.10.rows = bf16[16,96,384]{2,1,0:T(8,128)(2,1)S(1)} all-to-all(bf16[16,96,384]{2,1,0:T(8,128)(2,1)S(1)} %grid_product.1), channel_id=1, replica_groups=mesh['aa'=8,'ba'=16] {'ba'}, dimensions={0} | all-to-all | bytes 2359296 | tf_op jit(solution)/shard_map/all_to_all | solution.py:476
  63.4 2.0 %unpack.1 = (f32[32,16,384]{2,1,0:T(8,128)}, f32[32,16,384]{2,1,0:T(8,128)}, f32[32,16,384]{2,1,0:T(8,128)}) custom-call(bf16[16,96,384]{2,1,0:T(8,128)(2,1)S(1)} %all_to_all.10.rows), custom_call_target="tpu_custom_call" | custom-call | tf_op jit(solution)/shard_map/unpack/pallas_call | solution.py:447
  (5 shorter events, 0.0 us)
Async XLA Ops:
  0.6 22.5 %copy-start = (s32[8,160]{1,0:T(8,128)S(1)}, s32[8,160]{1,0:T(8,128)}, u32[]{:S(2)}) copy-start(s32[8,160]{1,0:T(8,128)} %orders.1) | copy-start | bytes 15364
  0.6 22.6 %copy-start.1 = (s32[9]{0:T(128)S(1)}, s32[9]{0:T(128)}, u32[]{:S(2)}) copy-start(s32[9]{0:T(128)} %limits.1) | copy-start | bytes 112
  0.7 24.9 %copy-start.2 = (s32[96]{0:T(128)S(1)}, s32[96]{0:T(128)}, u32[]{:S(2)}) copy-start(s32[96]{0:T(128)} %param.12) | copy-start | bytes 1156
  11.9 24.8 %all-to-all-start = ((bf16[128,16,128]{2,1,0:T(8,128)(2,1)}), bf16[128,16,128]{2,1,0:T(8,128)(2,1)S(1)}, u32[]{:S(2)}, u32[]{:S(2)}) async-start(bf16[128,16,128]{2,1,0:T(8,128)(2,1)} %wind_legendre.1), calls=%async_computation | async-start | bytes 1048576 | tf_op jit(solution)/shard_map/all_to_all | solution.py:469

commit v5 on v4

--- a/solution.py
+++ b/solution.py
@@ -23,9 +23,6 @@
 KM = 64
 KR = PAIRS - KM
 KALL = 2 * PAIRS + 1
-BLOCK = 16
-BLOCKS = PAIRS // BLOCK
-PART = BLOCK * MW
 AHEAD = 2
 F32 = jnp.float32
 BF16 = jnp.bfloat16
@@ -71,13 +68,13 @@
         yield pltpu.make_async_copy(pol.at[:, lanes], poly.at[:, lanes], sem_p.at[g])
 
     def copies(g):
-        return span(g, pl.multiple_of(g * PART + 128, 128), PART)
+        return span(g, pl.multiple_of(g * MAIN + 128, 128), MAIN)
 
     def first_copies():
-        return span(0, 0, PART + 128)
+        return span(0, 0, MAIN + 128)
 
     def last_copies():
-        return span(BLOCKS - 1, (BLOCKS - 1) * PART + 128, PART - 128)
+        return span(STEPS - 1, (STEPS - 1) * MAIN + 128, MAIN - 128)
 
     for copy in first_copies():
         copy.start()
@@ -97,22 +94,22 @@
         copy.wait()
 
     def turn(block):
-        @pl.when((block > 0) & (block < BLOCKS - 1))
+        @pl.when((block > 0) & (block < STEPS - 1))
         def _():
             for copy in copies(block):
                 copy.wait()
 
-        @pl.when(block == BLOCKS - 1)
+        @pl.when(block == STEPS - 1)
         def _():
             for copy in last_copies():
                 copy.wait()
 
-        @pl.when(block + AHEAD < BLOCKS - 1)
+        @pl.when(block + AHEAD < STEPS - 1)
         def _():
             for copy in copies(block + AHEAD):
                 copy.start()
 
-        @pl.when(block + AHEAD == BLOCKS - 1)
+        @pl.when(block + AHEAD == STEPS - 1)
         def _():
             for copy in last_copies():
                 copy.start()
@@ -126,6 +123,7 @@
 
 
 def one_group(step, turn, me, orders, poly, fields, coef_a, coef_b, coef_c, masks, north, south):
+    turn(step)
     origin = pl.multiple_of(step * MAIN, 128)
 
     lane = lax.broadcasted_iota(jnp.int32, (GROUP, WIN), 1)
@@ -176,8 +174,6 @@
 
     results = []
     for s in range(GROUP):
-        if s % BLOCK == 0:
-            turn(step * (GROUP // BLOCK) + s // BLOCK)
         window = pl.ds(pl.multiple_of(origin + s * MW, 128), WIN)
         both = fields[:, window].astype(F32)
         x, heat = both[0:8], both[8:16]
@@ -285,8 +281,8 @@
             pltpu.VMEM((12 * KALL, LATH), F32),
             pltpu.VMEM((12 * KALL, LATH), F32),
             pltpu.VMEM((2048, 128), F32),
-            pltpu.SemaphoreType.DMA((8, BLOCKS)),
-            pltpu.SemaphoreType.DMA((BLOCKS,)),
+            pltpu.SemaphoreType.DMA((8, STEPS)),
+            pltpu.SemaphoreType.DMA((STEPS,)),
         ],
         compiler_params=pltpu.CompilerParams(vmem_limit_bytes=40 * 1024 * 1024),
         name="wind_legendre",
@@ -352,6 +348,7 @@
 
 
 PSTEP = 4
+SENT = 248
 
 
 def grid_kernel(count, data, table, twist_c, twist_s, weight, out, f_re, f_im, twisted):
@@ -400,9 +397,20 @@
             ).astype(BF16)
     res = jnp.dot(twisted[...], table[...], preferred_element_type=F32)
     lon = lax.broadcasted_iota(jnp.int32, (96, PIECE), 1) * PIECES + step * PSTEP
+    left = lax.broadcasted_iota(jnp.int32, (48, 128), 1) < 64
+    pick_row = lax.broadcasted_iota(jnp.int32, (8, 128), 0) == 0
+    pick_col = lax.broadcasted_iota(jnp.int32, (8, 128), 1) == 64
+    pick = (pick_row & pick_col).astype(F32).astype(BF16)
     for u in range(PSTEP):
         keep = lon + u < count[0]
-        out[u] = jnp.where(keep, res[96 * u : 96 * u + 96], 0.0).astype(BF16)
+        val = jnp.where(keep, res[96 * u : 96 * u + 96], 0.0)
+        out[u, 0:96] = val[:, 0:128].astype(BF16)
+        out[u, 96:192] = val[:, 128:256].astype(BF16)
+        rest = val[:, 256:384]
+        out[u, 192:240] = jnp.where(left, rest[0:48], pltpu.roll(rest[48:96], 64, 1)).astype(BF16)
+        rest = jnp.concatenate([rest, jnp.zeros((32, 128), F32)], axis=0).astype(BF16)
+        last = lax.dot_general(pick, rest, NT, preferred_element_type=F32)
+        out[u, 240:SENT] = last.astype(BF16)
 
 
 def make_grid(count, data, tables):
@@ -420,8 +428,8 @@
             whole((PIECES, 1, MW)),
             whole((8, MW)),
         ],
-        out_specs=pl.BlockSpec((PSTEP, 96, PIECE), lambda i: (i, 0, 0)),
-        out_shape=jax.ShapeDtypeStruct((PIECES, 96, PIECE), BF16),
+        out_specs=pl.BlockSpec((PSTEP, SENT, 128), lambda i: (i, 0, 0)),
+        out_shape=jax.ShapeDtypeStruct((PIECES, SENT, 128), BF16),
         scratch_shapes=[
             pltpu.VMEM((96, MW), F32),
             pltpu.VMEM((96, MW), F32),
@@ -433,8 +441,30 @@
 
 
 def unpack_kernel(rows, out_u, out_v, out_t, wide):
-    for slot in range(BAND_MAX):
-        wide[97 * slot : 97 * slot + 96, :] = rows[slot].astype(F32)
+    step = pl.program_id(0)
+    for part in range(2):
+
+        @pl.when(step == part)
+        def _(part=part):
+            for slot in range(BAND_MAX):
+                chunk = rows[slot, 96 * part : 96 * part + 96]
+                wide[97 * slot : 97 * slot + 96, :] = chunk.astype(F32)
+
+    @pl.when(step == 2)
+    def _():
+        left = lax.broadcasted_iota(jnp.int32, (48, 128), 1) < 64
+        pick_row = lax.broadcasted_iota(jnp.int32, (8, 128), 0) == 0
+        pick_col = lax.broadcasted_iota(jnp.int32, (8, 128), 1) == 64
+        pick = (pick_row & pick_col).astype(F32).astype(BF16)
+        for slot in range(BAND_MAX):
+            both = rows[slot, 192:240].astype(F32)
+            last = lax.dot_general(
+                rows[slot, 240:SENT], pick, (((0,), (0,)), ((), ())), preferred_element_type=F32
+            )
+            for half, val in enumerate((both, pltpu.roll(both, 64, 1))):
+                val = jnp.where(left, val, 0.0) + last[48 * half : 48 * half + 48]
+                wide[97 * slot + 48 * half : 97 * slot + 48 * half + 48, :] = val
+
     for lv in range(2):
         for fld, out in enumerate((out_u, out_v, out_t)):
             for src in range(16):
@@ -447,7 +477,7 @@
     return pl.pallas_call(
         unpack_kernel,
         grid=(PIECE // 128,),
-        in_specs=[pl.BlockSpec((BAND_MAX, 96, 128), lambda i: (0, 0, i))],
+        in_specs=[pl.BlockSpec((BAND_MAX, SENT, 128), lambda i: (0, 0, 0))],
         out_specs=[pl.BlockSpec((LEVELS, BAND_MAX, 128), lambda i: (0, 0, i))] * 3,
         out_shape=[leaf] * 3,
         scratch_shapes=[pltpu.VMEM((BAND_MAX * 97, 128), F32)],

time: 65.7 us -> 64.3 us (0.979)
  blocking collectives: 21.3 us -> 19.3 us
    all_to_all x1, blocking collectives: 21.3 us -> 19.3 us  [per_device(): rows = lax.all_to_all(pieces, 'ba', split_axis=0, concat_axis=0, tiled=True)]
where the time goes in v5:
time: 64.3 us; the launch traced here: 64 us
  Pallas kernels  22.1 us (34%)
  blocking collectives  19.3 us (30%)
  starting transfers between devices  11.1 us (17%)
  waiting for transfers between devices  7.05 us (11%)
  between operations  2.68 us (4%)
  local copies, waits for them, and re-layouts  1.03 us (2%)
  other arithmetic  0.72 us (1%)
    all_to_all x1, blocking collectives, per_device(): rows = lax.all_to_all(pieces, 'ba', split_axis=0, concat_axis=0, tiled=True)  19.3 us
    all_to_all x1, starting transfers between devices, per_device(): lax.all_to_all(sent, ('aa', 'ba'), split_axis=0, concat_axis=0, tiled=True)  11.1 us
    pallas_call x1, Pallas kernels, wind_legendre(): pl.pallas_call(wind_legendre_kernel, grid=(1,), in_specs=[smem, smem, sme...  11.1 us
    all_to_all x1, waiting for transfers between devices, per_device(): lax.all_to_all(sent, ('aa', 'ba'), split_axis=0, concat_axis=0, tiled=True)  7.05 us
    pallas_call x1, Pallas kernels, make_grid(): pl.pallas_call(grid_kernel, grid=(PIECES // PSTEP,), in_specs=[pl.BlockSp...  5.91 us
    pallas_call x1, Pallas kernels, make_table(): pl.pallas_call(table_kernel, in_specs=[pl.BlockSpec(memory_space=pltpu.SM...  2.82 us
    pallas_call x1, Pallas kernels, unpack(): pl.pallas_call(unpack_kernel, grid=(PIECE // 128,), in_specs=[pl.BlockSpe...  2.28 us
  transfers between devices with their start and end apart: 1, of which 1 were waited for; matrix products, arithmetic and copies ran while one was open for 3% of the time, Pallas kernels for 4%

profile of v5, /device:TPU:0, one launch (start us, length us, event | category | flops | bytes accessed | tf_op | source)
XLA Modules:
  0.0 64.0 jit_solution(1605623598346601510)
XLA Ops:
  0.6 0.0 copy-start
  0.6 0.0 copy-start.1
  0.7 0.0 copy-start.2
  0.7 11.1 %wind_legendre.1 = bf16[128,16,128]{2,1,0:T(8,128)(2,1)} custom-call(s32[8,160]{1,0:T(8,128)} %orders.1, s32[9]{0:T(128)} %limits.1, s32[1]{0:T(128)} %bitcast.3.where_am_i, bf16[2,2,102480]{2,1,0:T(2,128)(2,1)} %rot_x.1, bf16[2,2,102480]{2,1,0:T(2,128)(2,1)} %dil_x.1, bf16[2,2,102480]{2,1,0:T(2,128)(2,1)} %tmp_x.1, bf16[48,102480]{1,0:T(8,128)(2,1)} %pol_x.1, ...), custom_call_target="tpu_custom_call" | custom-call | tf_op jit(solution)/shard_map/wind_legendre/pallas_call | solution.py:256
  11.7 11.1 %all-to-all-start = ((bf16[128,16,128]{2,1,0:T(8,128)(2,1)}), bf16[128,16,128]{2,1,0:T(8,128)(2,1)S(1)}, u32[]{:S(2)}, u32[]{:S(2)}) async-start(bf16[128,16,128]{2,1,0:T(8,128)(2,1)} %wind_legendre.1), calls=%async_computation | async-start | bytes 1048576 | tf_op jit(solution)/shard_map/all_to_all | solution.py:499
  22.9 0.0 copy-done
  22.9 0.2 slice.17
  23.0 0.0 copy-done.1
  23.1 0.1 dynamic_slice.3
  23.2 0.1 reshape.12
  23.2 0.1 pad_add_fusion
  23.3 0.1 reshape.13
  23.4 0.6 fusion.1
  25.3 0.0 copy-done.2
  25.3 0.6 fusion
  26.6 2.8 %trig_table.1 = (bf16[2560,384]{1,0:T(8,128)(2,1)S(1)}, f32[16,1,1280]{2,1,0:T(1,128)S(1)}, f32[16,1,1280]{2,1,0:T(1,128)S(1)}, f32[8,1280]{1,0:T(8,128)S(1)}) custom-call(s32[1]{0:T(128)} %bitcast.2.count, s32[1,1280]{1,0:T(1,128)S(1)} %pad_add_fusion.1.wave), custom_call_target="tpu_custom_call" | custom-call | flops 50000000 | bytes 4000000 | tf_op jit(solution)/shard_map/trig_table/pallas_call | solution.py:334
  29.4 7.0 %all-to-all-done.data = bf16[128,16,128]{2,1,0:T(8,128)(2,1)S(1)} async-done(((bf16[128,16,128]{2,1,0:T(8,128)(2,1)}), bf16[128,16,128]{2,1,0:T(8,128)(2,1)S(1)}, u32[]{:S(2)}, u32[]{:S(2)}) %all-to-all-start) | async-done | bytes 524320 | tf_op jit(solution)/shard_map/all_to_all | solution.py:499
  36.5 5.9 %grid_product.1 = bf16[16,248,128]{2,1,0:T(8,128)(2,1)S(1)} custom-call(s32[1]{0:T(128)} %bitcast.2.count, bf16[128,16,128]{2,1,0:T(8,128)(2,1)S(1)} %all-to-all-done.data, bf16[2560,384]{1,0:T(8,128)(2,1)S(1)} %get-tuple-element.7.table, f32[16,1,1280]{2,1,0:T(1,128)S(1)} %get-tuple-element.8.twist_c, f32[16,1,1280]{2,1,0:T(1,128)S(1)} %get-tuple-element.9.twist_s, ...), custom_call_target="tpu_custom_call" | custom-call | tf_op jit(solution)/shard_map/grid_product/pallas_call | solution.py:420
  42.4 19.3 %all_to_all.10.rows = bf16[16,248,128]{2,1,0:T(8,128)(2,1)S(1)} all-to-all(bf16[16,248,128]{2,1,0:T(8,128)(2,1)S(1)} %grid_product.1), channel_id=1, replica_groups=mesh['aa'=8,'ba'=16] {'ba'}, dimensions={0} | all-to-all | bytes 2031616 | tf_op jit(solution)/shard_map/all_to_all | solution.py:506
  61.7 2.3 %unpack.1 = (f32[32,16,384]{2,1,0:T(8,128)}, f32[32,16,384]{2,1,0:T(8,128)}, f32[32,16,384]{2,1,0:T(8,128)}) custom-call(bf16[16,248,128]{2,1,0:T(8,128)(2,1)S(1)} %all_to_all.10.rows), custom_call_target="tpu_custom_call" | custom-call | tf_op jit(solution)/shard_map/unpack/pallas_call | solution.py:477
  (5 shorter events, 0.0 us)
Async XLA Ops:
  0.6 22.2 %copy-start = (s32[8,160]{1,0:T(8,128)S(1)}, s32[8,160]{1,0:T(8,128)}, u32[]{:S(2)}) copy-start(s32[8,160]{1,0:T(8,128)} %orders.1) | copy-start | bytes 15364
  0.6 22.4 %copy-start.1 = (s32[9]{0:T(128)S(1)}, s32[9]{0:T(128)}, u32[]{:S(2)}) copy-start(s32[9]{0:T(128)} %limits.1) | copy-start | bytes 112
  0.7 24.6 %copy-start.2 = (s32[96]{0:T(128)S(1)}, s32[96]{0:T(128)}, u32[]{:S(2)}) copy-start(s32[96]{0:T(128)} %param.12) | copy-start | bytes 1156
  11.7 24.8 %all-to-all-start = ((bf16[128,16,128]{2,1,0:T(8,128)(2,1)}), bf16[128,16,128]{2,1,0:T(8,128)(2,1)S(1)}, u32[]{:S(2)}, u32[]{:S(2)}) async-start(bf16[128,16,128]{2,1,0:T(8,128)(2,1)} %wind_legendre.1), calls=%async_computation | async-start | bytes 1048576 | tf_op jit(solution)/shard_map/all_to_all | solution.py:499

commit v6 on v5

--- a/solution.py
+++ b/solution.py
@@ -347,7 +347,7 @@
     )(count, wave)
 
 
-PSTEP = 4
+PSTEP = 8
 SENT = 248
 
 

time: 64.3 us -> 63.6 us (0.989)
  Pallas kernels: 22.1 us -> 21.4 us
    pallas_call x1, Pallas kernels: 5.91 us -> 5.26 us  [make_grid(): pl.pallas_call(grid_kernel, grid=(PIECES // PSTEP,), in_specs=[pl.BlockSp...]
where the time goes in v6:
time: 63.6 us; the launch traced here: 63.4 us
  Pallas kernels  21.4 us (34%)
  blocking collectives  19.3 us (30%)
  starting transfers between devices  11.1 us (17%)
  waiting for transfers between devices  7.05 us (11%)
  between operations  2.68 us (4%)
  local copies, waits for them, and re-layouts  1.03 us (2%)
  other arithmetic  0.72 us (1%)
    all_to_all x1, blocking collectives, per_device(): rows = lax.all_to_all(pieces, 'ba', split_axis=0, concat_axis=0, tiled=True)  19.3 us
    all_to_all x1, starting transfers between devices, per_device(): lax.all_to_all(sent, ('aa', 'ba'), split_axis=0, concat_axis=0, tiled=True)  11.1 us
    pallas_call x1, Pallas kernels, wind_legendre(): pl.pallas_call(wind_legendre_kernel, grid=(1,), in_specs=[smem, smem, sme...  11.1 us
    all_to_all x1, waiting for transfers between devices, per_device(): lax.all_to_all(sent, ('aa', 'ba'), split_axis=0, concat_axis=0, tiled=True)  7.05 us
    pallas_call x1, Pallas kernels, make_grid(): pl.pallas_call(grid_kernel, grid=(PIECES // PSTEP,), in_specs=[pl.BlockSp...  5.26 us
    pallas_call x1, Pallas kernels, make_table(): pl.pallas_call(table_kernel, in_specs=[pl.BlockSpec(memory_space=pltpu.SM...  2.82 us
    pallas_call x1, Pallas kernels, unpack(): pl.pallas_call(unpack_kernel, grid=(PIECE // 128,), in_specs=[pl.BlockSpe...  2.28 us
  transfers between devices with their start and end apart: 1, of which 1 were waited for; matrix products, arithmetic and copies ran while one was open for 3% of the time, Pallas kernels for 4%

profile of v6, /device:TPU:0, one launch (start us, length us, event | category | flops | bytes accessed | tf_op | source)
XLA Modules:
  0.0 63.4 jit_solution(15228146486968294318)
XLA Ops:
  0.6 0.0 copy-start
  0.6 0.0 copy-start.1
  0.7 0.0 copy-start.2
  0.7 11.1 %wind_legendre.1 = bf16[128,16,128]{2,1,0:T(8,128)(2,1)} custom-call(s32[8,160]{1,0:T(8,128)} %orders.1, s32[9]{0:T(128)} %limits.1, s32[1]{0:T(128)} %bitcast.3.where_am_i, bf16[2,2,102480]{2,1,0:T(2,128)(2,1)} %rot_x.1, bf16[2,2,102480]{2,1,0:T(2,128)(2,1)} %dil_x.1, bf16[2,2,102480]{2,1,0:T(2,128)(2,1)} %tmp_x.1, bf16[48,102480]{1,0:T(8,128)(2,1)} %pol_x.1, ...), custom_call_target="tpu_custom_call" | custom-call | tf_op jit(solution)/shard_map/wind_legendre/pallas_call | solution.py:256
  11.7 11.1 %all-to-all-start = ((bf16[128,16,128]{2,1,0:T(8,128)(2,1)}), bf16[128,16,128]{2,1,0:T(8,128)(2,1)S(1)}, u32[]{:S(2)}, u32[]{:S(2)}) async-start(bf16[128,16,128]{2,1,0:T(8,128)(2,1)} %wind_legendre.1), calls=%async_computation | async-start | bytes 1048576 | tf_op jit(solution)/shard_map/all_to_all | solution.py:499
  22.9 0.0 copy-done
  22.9 0.2 slice.17
  23.0 0.0 copy-done.1
  23.1 0.1 dynamic_slice.3
  23.2 0.1 reshape.12
  23.2 0.1 pad_add_fusion
  23.3 0.1 reshape.13
  23.4 0.6 fusion.1
  25.3 0.0 copy-done.2
  25.3 0.6 fusion
  26.6 2.8 %trig_table.1 = (bf16[2560,384]{1,0:T(8,128)(2,1)S(1)}, f32[16,1,1280]{2,1,0:T(1,128)S(1)}, f32[16,1,1280]{2,1,0:T(1,128)S(1)}, f32[8,1280]{1,0:T(8,128)S(1)}) custom-call(s32[1]{0:T(128)} %bitcast.2.count, s32[1,1280]{1,0:T(1,128)S(1)} %pad_add_fusion.1.wave), custom_call_target="tpu_custom_call" | custom-call | flops 50000000 | bytes 4000000 | tf_op jit(solution)/shard_map/trig_table/pallas_call | solution.py:334
  29.4 7.0 %all-to-all-done.data = bf16[128,16,128]{2,1,0:T(8,128)(2,1)S(1)} async-done(((bf16[128,16,128]{2,1,0:T(8,128)(2,1)}), bf16[128,16,128]{2,1,0:T(8,128)(2,1)S(1)}, u32[]{:S(2)}, u32[]{:S(2)}) %all-to-all-start) | async-done | bytes 524320 | tf_op jit(solution)/shard_map/all_to_all | solution.py:499
  36.5 5.3 %grid_product.1 = bf16[16,248,128]{2,1,0:T(8,128)(2,1)S(1)} custom-call(s32[1]{0:T(128)} %bitcast.2.count, bf16[128,16,128]{2,1,0:T(8,128)(2,1)S(1)} %all-to-all-done.data, bf16[2560,384]{1,0:T(8,128)(2,1)S(1)} %get-tuple-element.7.table, f32[16,1,1280]{2,1,0:T(1,128)S(1)} %get-tuple-element.8.twist_c, f32[16,1,1280]{2,1,0:T(1,128)S(1)} %get-tuple-element.9.twist_s, ...), custom_call_target="tpu_custom_call" | custom-call | tf_op jit(solution)/shard_map/grid_product/pallas_call | solution.py:420
  41.8 19.3 %all_to_all.10.rows = bf16[16,248,128]{2,1,0:T(8,128)(2,1)S(1)} all-to-all(bf16[16,248,128]{2,1,0:T(8,128)(2,1)S(1)} %grid_product.1), channel_id=1, replica_groups=mesh['aa'=8,'ba'=16] {'ba'}, dimensions={0} | all-to-all | bytes 2031616 | tf_op jit(solution)/shard_map/all_to_all | solution.py:506
  61.1 2.3 %unpack.1 = (f32[32,16,384]{2,1,0:T(8,128)}, f32[32,16,384]{2,1,0:T(8,128)}, f32[32,16,384]{2,1,0:T(8,128)}) custom-call(bf16[16,248,128]{2,1,0:T(8,128)(2,1)S(1)} %all_to_all.10.rows), custom_call_target="tpu_custom_call" | custom-call | tf_op jit(solution)/shard_map/unpack/pallas_call | solution.py:477
  (5 shorter events, 0.0 us)
Async XLA Ops:
  0.6 22.2 %copy-start = (s32[8,160]{1,0:T(8,128)S(1)}, s32[8,160]{1,0:T(8,128)}, u32[]{:S(2)}) copy-start(s32[8,160]{1,0:T(8,128)} %orders.1) | copy-start | bytes 15364
  0.6 22.4 %copy-start.1 = (s32[9]{0:T(128)S(1)}, s32[9]{0:T(128)}, u32[]{:S(2)}) copy-start(s32[9]{0:T(128)} %limits.1) | copy-start | bytes 112
  0.7 24.6 %copy-start.2 = (s32[96]{0:T(128)S(1)}, s32[96]{0:T(128)}, u32[]{:S(2)}) copy-start(s32[96]{0:T(128)} %param.12) | copy-start | bytes 1156
  11.7 24.8 %all-to-all-start = ((bf16[128,16,128]{2,1,0:T(8,128)(2,1)}), bf16[128,16,128]{2,1,0:T(8,128)(2,1)S(1)}, u32[]{:S(2)}, u32[]{:S(2)}) async-start(bf16[128,16,128]{2,1,0:T(8,128)(2,1)} %wind_legendre.1), calls=%async_computation | async-start | bytes 1048576 | tf_op jit(solution)/shard_map/all_to_all | solution.py:499

commit v7 on v6

--- a/solution.py
+++ b/solution.py
@@ -24,6 +24,7 @@
 KR = PAIRS - KM
 KALL = 2 * PAIRS + 1
 AHEAD = 2
+PITCH = 17
 F32 = jnp.float32
 BF16 = jnp.bfloat16
 NT = (((1,), (1,)), ((), ()))
@@ -219,7 +220,7 @@
         val = lax.dot_general(pick_n, rows_n, NT, preferred_element_type=F32)
         val = val + lax.dot_general(pick_s, rows_s, NT, preferred_element_type=F32)
         for block in range(16):
-            tiles[pl.ds(row + 128 * block, 8, stride=16), :] = val[8 * block : 8 * block + 8]
+            tiles[pl.ds(row + 8 * PITCH * block, 8, stride=PITCH), :] = val[8 * block : 8 * block + 8]
 
     for part in range(2):
         for lv in range(2):
@@ -240,10 +241,10 @@
             )
         select(both[0], both[1], 12 + fld)
     for block in range(16):
-        tiles[pl.ds(15 + 128 * block, 8, stride=16), :] = jnp.zeros((8, 128), F32)
+        tiles[pl.ds(15 + 8 * PITCH * block, 8, stride=PITCH), :] = jnp.zeros((8, 128), F32)
     for block in range(16):
-        part = tiles[128 * block : 128 * block + 128, :]
-        out[8 * block : 8 * block + 8] = part.reshape(8, 16, 128).astype(BF16)
+        for dst in range(8 * block, 8 * block + 8):
+            out[dst] = tiles[PITCH * dst : PITCH * dst + 16, :].astype(BF16)
 
 
 def wind_legendre(rot, dil, tmp, pol, orders, limits, me):
@@ -280,7 +281,7 @@
             pltpu.VMEM((2, GROUP, WIN), F32),
             pltpu.VMEM((12 * KALL, LATH), F32),
             pltpu.VMEM((12 * KALL, LATH), F32),
-            pltpu.VMEM((2048, 128), F32),
+            pltpu.VMEM((128 * PITCH, 128), F32),
             pltpu.SemaphoreType.DMA((8, STEPS)),
             pltpu.SemaphoreType.DMA((STEPS,)),
         ],

time: 63.6 us -> 63.6 us (level)
  no operation moved by 1% of the time
where the time goes in v7:
time: 63.6 us; the launch traced here: 63.3 us
  Pallas kernels  21.3 us (33%)
  blocking collectives  19.3 us (30%)
  starting transfers between devices  11.1 us (17%)
  waiting for transfers between devices  7.05 us (11%)
  between operations  2.68 us (4%)
  local copies, waits for them, and re-layouts  1.03 us (2%)
  other arithmetic  0.72 us (1%)
    all_to_all x1, blocking collectives, per_device(): rows = lax.all_to_all(pieces, 'ba', split_axis=0, concat_axis=0, tiled=True)  19.3 us
    all_to_all x1, starting transfers between devices, per_device(): lax.all_to_all(sent, ('aa', 'ba'), split_axis=0, concat_axis=0, tiled=True)  11.1 us
    pallas_call x1, Pallas kernels, wind_legendre(): pl.pallas_call(wind_legendre_kernel, grid=(1,), in_specs=[smem, smem, sme...  11 us
    all_to_all x1, waiting for transfers between devices, per_device(): lax.all_to_all(sent, ('aa', 'ba'), split_axis=0, concat_axis=0, tiled=True)  7.05 us
    pallas_call x1, Pallas kernels, make_grid(): pl.pallas_call(grid_kernel, grid=(PIECES // PSTEP,), in_specs=[pl.BlockSp...  5.26 us
    pallas_call x1, Pallas kernels, make_table(): pl.pallas_call(table_kernel, in_specs=[pl.BlockSpec(memory_space=pltpu.SM...  2.82 us
    pallas_call x1, Pallas kernels, unpack(): pl.pallas_call(unpack_kernel, grid=(PIECE // 128,), in_specs=[pl.BlockSpe...  2.28 us
  transfers between devices with their start and end apart: 1, of which 1 were waited for; matrix products, arithmetic and copies ran while one was open for 3% of the time, Pallas kernels for 4%

profile of v7, /device:TPU:0, one launch (start us, length us, event | category | flops | bytes accessed | tf_op | source)
XLA Modules:
  0.0 63.3 jit_solution(15907365846482219317)
XLA Ops:
  0.6 0.0 copy-start
  0.6 0.0 copy-start.1
  0.7 0.0 copy-start.2
  0.7 11.0 %wind_legendre.1 = bf16[128,16,128]{2,1,0:T(8,128)(2,1)} custom-call(s32[8,160]{1,0:T(8,128)} %orders.1, s32[9]{0:T(128)} %limits.1, s32[1]{0:T(128)} %bitcast.3.where_am_i, bf16[2,2,102480]{2,1,0:T(2,128)(2,1)} %rot_x.1, bf16[2,2,102480]{2,1,0:T(2,128)(2,1)} %dil_x.1, bf16[2,2,102480]{2,1,0:T(2,128)(2,1)} %tmp_x.1, bf16[48,102480]{1,0:T(8,128)(2,1)} %pol_x.1, ...), custom_call_target="tpu_custom_call" | custom-call | tf_op jit(solution)/shard_map/wind_legendre/pallas_call | solution.py:257
  11.6 11.1 %all-to-all-start = ((bf16[128,16,128]{2,1,0:T(8,128)(2,1)}), bf16[128,16,128]{2,1,0:T(8,128)(2,1)S(1)}, u32[]{:S(2)}, u32[]{:S(2)}) async-start(bf16[128,16,128]{2,1,0:T(8,128)(2,1)} %wind_legendre.1), calls=%async_computation | async-start | bytes 1048576 | tf_op jit(solution)/shard_map/all_to_all | solution.py:500
  22.8 0.0 copy-done
  22.8 0.2 slice.17
  23.0 0.0 copy-done.1
  23.0 0.1 dynamic_slice.3
  23.1 0.1 reshape.12
  23.2 0.1 pad_add_fusion
  23.2 0.1 reshape.13
  23.3 0.6 fusion.1
  25.2 0.0 copy-done.2
  25.2 0.6 fusion
  26.5 2.8 %trig_table.1 = (bf16[2560,384]{1,0:T(8,128)(2,1)S(1)}, f32[16,1,1280]{2,1,0:T(1,128)S(1)}, f32[16,1,1280]{2,1,0:T(1,128)S(1)}, f32[8,1280]{1,0:T(8,128)S(1)}) custom-call(s32[1]{0:T(128)} %bitcast.2.count, s32[1,1280]{1,0:T(1,128)S(1)} %pad_add_fusion.1.wave), custom_call_target="tpu_custom_call" | custom-call | flops 50000000 | bytes 4000000 | tf_op jit(solution)/shard_map/trig_table/pallas_call | solution.py:335
  29.3 7.0 %all-to-all-done.data = bf16[128,16,128]{2,1,0:T(8,128)(2,1)S(1)} async-done(((bf16[128,16,128]{2,1,0:T(8,128)(2,1)}), bf16[128,16,128]{2,1,0:T(8,128)(2,1)S(1)}, u32[]{:S(2)}, u32[]{:S(2)}) %all-to-all-start) | async-done | bytes 524320 | tf_op jit(solution)/shard_map/all_to_all | solution.py:500
  36.4 5.3 %grid_product.1 = bf16[16,248,128]{2,1,0:T(8,128)(2,1)S(1)} custom-call(s32[1]{0:T(128)} %bitcast.2.count, bf16[128,16,128]{2,1,0:T(8,128)(2,1)S(1)} %all-to-all-done.data, bf16[2560,384]{1,0:T(8,128)(2,1)S(1)} %get-tuple-element.7.table, f32[16,1,1280]{2,1,0:T(1,128)S(1)} %get-tuple-element.8.twist_c, f32[16,1,1280]{2,1,0:T(1,128)S(1)} %get-tuple-element.9.twist_s, ...), custom_call_target="tpu_custom_call" | custom-call | tf_op jit(solution)/shard_map/grid_product/pallas_call | solution.py:421
  41.7 19.3 %all_to_all.10.rows = bf16[16,248,128]{2,1,0:T(8,128)(2,1)S(1)} all-to-all(bf16[16,248,128]{2,1,0:T(8,128)(2,1)S(1)} %grid_product.1), channel_id=1, replica_groups=mesh['aa'=8,'ba'=16] {'ba'}, dimensions={0} | all-to-all | bytes 2031616 | tf_op jit(solution)/shard_map/all_to_all | solution.py:507
  61.0 2.3 %unpack.1 = (f32[32,16,384]{2,1,0:T(8,128)}, f32[32,16,384]{2,1,0:T(8,128)}, f32[32,16,384]{2,1,0:T(8,128)}) custom-call(bf16[16,248,128]{2,1,0:T(8,128)(2,1)S(1)} %all_to_all.10.rows), custom_call_target="tpu_custom_call" | custom-call | tf_op jit(solution)/shard_map/unpack/pallas_call | solution.py:478
  (5 shorter events, 0.0 us)
Async XLA Ops:
  0.6 22.2 %copy-start = (s32[8,160]{1,0:T(8,128)S(1)}, s32[8,160]{1,0:T(8,128)}, u32[]{:S(2)}) copy-start(s32[8,160]{1,0:T(8,128)} %orders.1) | copy-start | bytes 15364
  0.6 22.3 %copy-start.1 = (s32[9]{0:T(128)S(1)}, s32[9]{0:T(128)}, u32[]{:S(2)}) copy-start(s32[9]{0:T(128)} %limits.1) | copy-start | bytes 112
  0.7 24.6 %copy-start.2 = (s32[96]{0:T(128)S(1)}, s32[96]{0:T(128)}, u32[]{:S(2)}) copy-start(s32[96]{0:T(128)} %param.12) | copy-start | bytes 1156
  11.6 24.8 %all-to-all-start = ((bf16[128,16,128]{2,1,0:T(8,128)(2,1)}), bf16[128,16,128]{2,1,0:T(8,128)(2,1)S(1)}, u32[]{:S(2)}, u32[]{:S(2)}) async-start(bf16[128,16,128]{2,1,0:T(8,128)(2,1)} %wind_legendre.1), calls=%async_computation | async-start | bytes 1048576 | tf_op jit(solution)/shard_map/all_to_all | solution.py:500

commit v8 on v6

--- a/solution.py
+++ b/solution.py
@@ -360,16 +360,17 @@
         col = lax.broadcasted_iota(jnp.int32, (192, 256), 1)
         pick_main = (col == (row % 16) * 16 + row // 16).astype(F32).astype(BF16)
         pick_rest = (col == (row % 16) * 16 + 12 + (row // 16) % 3).astype(F32).astype(BF16)
+        picks = jnp.concatenate([pick_main, pick_rest], axis=0)
         lane = lax.broadcasted_iota(jnp.int32, (48, 128), 1) // 32
         rest = [[jnp.zeros((48, 128), F32) for _ in range(2)] for _ in range(4)]
         for a in range(8):
             x = data[16 * a : 16 * a + 16].reshape(256, 128)
             lanes = slice(128 * a, 128 * a + 128)
             w = weight[0:1, lanes]
-            main = jnp.dot(pick_main, x, preferred_element_type=F32)
+            picked = jnp.dot(picks, x, preferred_element_type=F32)
+            main, more = picked[0:192], picked[192:384]
             f_re[:, lanes] = main[0:96] * w
             f_im[:, lanes] = main[96:192] * w
-            more = jnp.dot(pick_rest, x, preferred_element_type=F32)
             for q in range(4):
                 piece = more[48 * q : 48 * q + 48]
                 shift = (32 * (a % 4) - 32 * q) % 128

time: 63.6 us -> 63.7 us (level)
  no operation moved by 1% of the time
where the time goes in v8:
time: 63.7 us; the launch traced here: 63.4 us
  Pallas kernels  21.5 us (34%)
  blocking collectives  19.3 us (30%)
  starting transfers between devices  11.1 us (17%)
  waiting for transfers between devices  7.05 us (11%)
  between operations  2.68 us (4%)
  local copies, waits for them, and re-layouts  1.03 us (2%)
  other arithmetic  0.72 us (1%)
    all_to_all x1, blocking collectives, per_device(): rows = lax.all_to_all(pieces, 'ba', split_axis=0, concat_axis=0, tiled=True)  19.3 us
    all_to_all x1, starting transfers between devices, per_device(): lax.all_to_all(sent, ('aa', 'ba'), split_axis=0, concat_axis=0, tiled=True)  11.1 us
    pallas_call x1, Pallas kernels, wind_legendre(): pl.pallas_call(wind_legendre_kernel, grid=(1,), in_specs=[smem, smem, sme...  11.1 us
    all_to_all x1, waiting for transfers between devices, per_device(): lax.all_to_all(sent, ('aa', 'ba'), split_axis=0, concat_axis=0, tiled=True)  7.05 us
    pallas_call x1, Pallas kernels, make_grid(): pl.pallas_call(grid_kernel, grid=(PIECES // PSTEP,), in_specs=[pl.BlockSp...  5.31 us
    pallas_call x1, Pallas kernels, make_table(): pl.pallas_call(table_kernel, in_specs=[pl.BlockSpec(memory_space=pltpu.SM...  2.82 us
    pallas_call x1, Pallas kernels, unpack(): pl.pallas_call(unpack_kernel, grid=(PIECE // 128,), in_specs=[pl.BlockSpe...  2.28 us
  transfers between devices with their start and end apart: 1, of which 1 were waited for; matrix products, arithmetic and copies ran while one was open for 3% of the time, Pallas kernels for 4%

profile of v8, /device:TPU:0, one launch (start us, length us, event | category | flops | bytes accessed | tf_op | source)
XLA Modules:
  0.0 63.4 jit_solution(7134693751731548925)
XLA Ops:
  0.6 0.0 copy-start
  0.6 0.0 copy-start.1
  0.7 0.0 copy-start.2
  0.7 11.1 %wind_legendre.1 = bf16[128,16,128]{2,1,0:T(8,128)(2,1)} custom-call(s32[8,160]{1,0:T(8,128)} %orders.1, s32[9]{0:T(128)} %limits.1, s32[1]{0:T(128)} %bitcast.3.where_am_i, bf16[2,2,102480]{2,1,0:T(2,128)(2,1)} %rot_x.1, bf16[2,2,102480]{2,1,0:T(2,128)(2,1)} %dil_x.1, bf16[2,2,102480]{2,1,0:T(2,128)(2,1)} %tmp_x.1, bf16[48,102480]{1,0:T(8,128)(2,1)} %pol_x.1, ...), custom_call_target="tpu_custom_call" | custom-call | tf_op jit(solution)/shard_map/wind_legendre/pallas_call | solution.py:256
  11.7 11.1 %all-to-all-start = ((bf16[128,16,128]{2,1,0:T(8,128)(2,1)}), bf16[128,16,128]{2,1,0:T(8,128)(2,1)S(1)}, u32[]{:S(2)}, u32[]{:S(2)}) async-start(bf16[128,16,128]{2,1,0:T(8,128)(2,1)} %wind_legendre.1), calls=%async_computation | async-start | bytes 1048576 | tf_op jit(solution)/shard_map/all_to_all | solution.py:500
  22.9 0.0 copy-done
  22.9 0.2 slice.17
  23.0 0.0 copy-done.1
  23.1 0.1 dynamic_slice.3
  23.2 0.1 reshape.12
  23.2 0.1 pad_add_fusion
  23.3 0.1 reshape.13
  23.4 0.6 fusion.1
  25.3 0.0 copy-done.2
  25.3 0.6 fusion
  26.6 2.8 %trig_table.1 = (bf16[2560,384]{1,0:T(8,128)(2,1)S(1)}, f32[16,1,1280]{2,1,0:T(1,128)S(1)}, f32[16,1,1280]{2,1,0:T(1,128)S(1)}, f32[8,1280]{1,0:T(8,128)S(1)}) custom-call(s32[1]{0:T(128)} %bitcast.2.count, s32[1,1280]{1,0:T(1,128)S(1)} %pad_add_fusion.1.wave), custom_call_target="tpu_custom_call" | custom-call | flops 50000000 | bytes 4000000 | tf_op jit(solution)/shard_map/trig_table/pallas_call | solution.py:334
  29.4 7.0 %all-to-all-done.data = bf16[128,16,128]{2,1,0:T(8,128)(2,1)S(1)} async-done(((bf16[128,16,128]{2,1,0:T(8,128)(2,1)}), bf16[128,16,128]{2,1,0:T(8,128)(2,1)S(1)}, u32[]{:S(2)}, u32[]{:S(2)}) %all-to-all-start) | async-done | bytes 524320 | tf_op jit(solution)/shard_map/all_to_all | solution.py:500
  36.5 5.3 %grid_product.1 = bf16[16,248,128]{2,1,0:T(8,128)(2,1)S(1)} custom-call(s32[1]{0:T(128)} %bitcast.2.count, bf16[128,16,128]{2,1,0:T(8,128)(2,1)S(1)} %all-to-all-done.data, bf16[2560,384]{1,0:T(8,128)(2,1)S(1)} %get-tuple-element.7.table, f32[16,1,1280]{2,1,0:T(1,128)S(1)} %get-tuple-element.8.twist_c, f32[16,1,1280]{2,1,0:T(1,128)S(1)} %get-tuple-element.9.twist_s, ...), custom_call_target="tpu_custom_call" | custom-call | tf_op jit(solution)/shard_map/grid_product/pallas_call | solution.py:421
  41.8 19.3 %all_to_all.10.rows = bf16[16,248,128]{2,1,0:T(8,128)(2,1)S(1)} all-to-all(bf16[16,248,128]{2,1,0:T(8,128)(2,1)S(1)} %grid_product.1), channel_id=1, replica_groups=mesh['aa'=8,'ba'=16] {'ba'}, dimensions={0} | all-to-all | bytes 2031616 | tf_op jit(solution)/shard_map/all_to_all | solution.py:507
  61.1 2.3 %unpack.1 = (f32[32,16,384]{2,1,0:T(8,128)}, f32[32,16,384]{2,1,0:T(8,128)}, f32[32,16,384]{2,1,0:T(8,128)}) custom-call(bf16[16,248,128]{2,1,0:T(8,128)(2,1)S(1)} %all_to_all.10.rows), custom_call_target="tpu_custom_call" | custom-call | tf_op jit(solution)/shard_map/unpack/pallas_call | solution.py:478
  (5 shorter events, 0.0 us)
Async XLA Ops:
  0.6 22.2 %copy-start = (s32[8,160]{1,0:T(8,128)S(1)}, s32[8,160]{1,0:T(8,128)}, u32[]{:S(2)}) copy-start(s32[8,160]{1,0:T(8,128)} %orders.1) | copy-start | bytes 15364
  0.6 22.4 %copy-start.1 = (s32[9]{0:T(128)S(1)}, s32[9]{0:T(128)}, u32[]{:S(2)}) copy-start(s32[9]{0:T(128)} %limits.1) | copy-start | bytes 112
  0.7 24.6 %copy-start.2 = (s32[96]{0:T(128)S(1)}, s32[96]{0:T(128)}, u32[]{:S(2)}) copy-start(s32[96]{0:T(128)} %param.12) | copy-start | bytes 1156
  11.7 24.8 %all-to-all-start = ((bf16[128,16,128]{2,1,0:T(8,128)(2,1)}), bf16[128,16,128]{2,1,0:T(8,128)(2,1)S(1)}, u32[]{:S(2)}, u32[]{:S(2)}) async-start(bf16[128,16,128]{2,1,0:T(8,128)(2,1)} %wind_legendre.1), calls=%async_computation | async-start | bytes 1048576 | tf_op jit(solution)/shard_map/all_to_all | solution.py:500
